TPU v7x, 256 devices: a whole 4x4x8 slice. The times are simulated.
256 devices in a mesh: gz: 8 (over z), gy: 8 (over y, core), gx: 4 (over x).
Axes of the slice: x: 4, y: 4, z: 8, core: 2. Of those that a mesh axis runs over, the one named last changes fastest.
Arguments:
- side_field: float32 [2, 384, 256, 512], P(None, 'gz', 'gy', 'gx'), may hold values from -6 to 6
- magnetogram: float32 [256, 512], P('gy', 'gx'), may hold values from -6 to 6
Outputs:
- potential: float32 [3, 384, 256, 512], P(None, 'gz', 'gy', 'gx')
All inputs are finite; a program needn't handle non-finite values.
Results may differ from a plain program's by a relative error of at most 0.000021.
Values sent between devices are 32-bit elements; how exact they have to be, the bound alone decides.
A program may use at most 64 MiB of HBM per device.

v0:
```python
import jax
import jax.numpy as jnp
from jax import lax
from jax.sharding import PartitionSpec as P

spacing = 0.0625
friction = 0.004


def from_everyone(shard, axis):
    copies = jnp.broadcast_to(shard, (lax.axis_size(axis), *shard.shape))
    return lax.all_to_all(copies, axis, split_axis=0, concat_axis=0, tiled=True)


def combined_pairwise(pieces, combine):
    while len(jax.tree.leaves(pieces)[0]) > 1:
        pieces = jax.vmap(combine)(*(pieces[side::2] for side in (0, 1)))
    return pieces[0]


def carried_in(shard, axis, combine, identity):
    size, here = (lax.axis_size(axis), lax.axis_index(axis))
    passed = jnp.arange(size) < here

    def kept(part, zero, own):
        part = jnp.where(
            passed.reshape(-1, *(1 for _ in own.shape)), part, jnp.asarray(zero, own.dtype)
        )
        return part

    pieces = from_everyone(shard, axis)
    return combined_pairwise(kept(pieces, identity, shard), combine)


def joined_along(tiles, dim):
    tiles = jnp.moveaxis(tiles, 0, dim)
    dims = tiles.shape
    return tiles.reshape(*dims[:dim], dims[dim] * dims[dim + 1], *dims[dim + 2 :])


def collect(shard, axis, dim):
    return joined_along(from_everyone(shard, axis), dim)


def with_halo(block, sides, width):
    for axis, dim in sides:
        count = lax.axis_size(axis)
        forward = [(i, i + 1) for i in range(count - 1)]
        backward = [(target, source) for source, target in forward]
        low = lax.ppermute(
            lax.slice_in_dim(block, block.shape[dim] - width, None, axis=dim), axis, forward
        )
        high = lax.ppermute(lax.slice_in_dim(block, 0, width, axis=dim), axis, backward)
        block = jnp.concatenate([low, block, high], axis=dim)
    return block


def forward_parts(values):
    anchor = values[:-1, :-1, :-1]
    return (
        values[1:, :-1, :-1] - anchor,
        values[:-1, 1:, :-1] - anchor,
        values[:-1, :-1, 1:] - anchor,
    )


def backward_parts(values):
    corner = values[1:, 1:, 1:]
    return (
        corner - values[:-1, 1:, 1:],
        corner - values[1:, :-1, 1:],
        corner - values[1:, 1:, :-1],
    )


def advance(padded):
    along_x = forward_parts(padded[0])
    along_y = forward_parts(padded[1])
    along_z = forward_parts(padded[2])
    field_x = (along_z[1] - along_y[0]) / spacing
    field_y = (along_x[0] - along_z[2]) / spacing
    field_z = (along_y[2] - along_x[1]) / spacing
    back_x = backward_parts(field_x)
    back_y = backward_parts(field_y)
    back_z = backward_parts(field_z)
    current_x = (back_z[1] - back_y[0]) / spacing
    current_y = (back_x[0] - back_z[2]) / spacing
    current_z = (back_y[2] - back_x[1]) / spacing
    cell_x = field_x[1:, 1:, 1:]
    cell_y = field_y[1:, 1:, 1:]
    cell_z = field_z[1:, 1:, 1:]
    denominator = cell_x * cell_x + cell_y * cell_y + cell_z * cell_z + 1.0
    speed_x = (current_y * cell_z - current_z * cell_y) / denominator
    speed_y = (current_z * cell_x - current_x * cell_z) / denominator
    speed_z = (current_x * cell_y - current_y * cell_x) / denominator
    drive_x = speed_y * cell_z - speed_z * cell_y
    drive_y = speed_z * cell_x - speed_x * cell_z
    drive_z = speed_x * cell_y - speed_y * cell_x
    inner = padded[:, 1:-1, 1:-1, 1:-1]
    return inner + friction * jnp.stack([drive_x, drive_y, drive_z])


def add_up(earlier, later):
    return earlier + later


def inside(count, device_index, device_count):
    first = device_index * count - 1
    position = first + jnp.arange(count + 2, dtype=jnp.int32)
    return ((position >= 0) & (position < count * device_count)).astype(jnp.float32)


def local(side_field, magnetogram):
    half = 0.5 * spacing
    rows_sum = jnp.cumsum(magnetogram, axis=1)
    row_totals = rows_sum[:, -1]
    row_carry = carried_in(row_totals, "gx", add_up, jnp.zeros_like(row_totals))
    base_y = half * (rows_sum + row_carry[:, None])
    columns_sum = jnp.cumsum(magnetogram, axis=0)
    column_totals = columns_sum[-1]
    column_carry = carried_in(column_totals, "gy", add_up, jnp.zeros_like(column_totals))
    base_x = -half * (columns_sum + column_carry[None, :])
    vertical = jnp.cumsum(side_field, axis=1)
    totals = vertical[:, -1]
    everyone = collect(totals[None], "gz", 0)
    lower = (jnp.arange(everyone.shape[0], dtype=jnp.int32) < lax.axis_index("gz")).astype(
        jnp.float32
    )
    below = jnp.sum(lower[:, None, None, None] * everyone, axis=0)
    rising = vertical + below[:, None]
    potential = jnp.stack(
        [
            base_x[None] + spacing * rising[1],
            base_y[None] - spacing * rising[0],
            jnp.zeros_like(rising[0]),
        ]
    )
    depth_z, depth_y, depth_x = (potential.shape[1], potential.shape[2], potential.shape[3])
    width = 2
    sides = with_halo(potential[:2], (("gz", 1), ("gy", 2), ("gx", 3)), width)
    padded = jnp.concatenate([sides, jnp.zeros_like(sides[:1])], axis=0)
    widened = advance(padded)
    mask_z = inside(depth_z, lax.axis_index("gz"), lax.axis_size("gz"))
    mask_y = inside(depth_y, lax.axis_index("gy"), lax.axis_size("gy"))
    mask_x = inside(depth_x, lax.axis_index("gx"), lax.axis_size("gx"))
    valid = mask_z[:, None, None] * mask_y[None, :, None] * mask_x[None, None, :]
    widened = widened * valid[None]
    potential = advance(widened)
    return potential


def solution(mesh):
    return jax.shard_map(
        local,
        mesh=mesh,
        in_specs=(P(None, "gz", "gy", "gx"), P("gy", "gx")),
        out_specs=P(None, "gz", "gy", "gx"),
        check_vma=False,
    )
```

profile of v0, /device:TPU:1, one launch (start us, length us, event | category | flops | bytes accessed | tf_op | source)
XLA Modules:
  0.0 121.0 jit_solution(14112978129399771909)
XLA Ops:
  1.9 4.8 %all-to-all-start.2 = ((f32[4,1,32]{2,1,0:T(1,128)}), f32[4,1,32]{2,1,0:T(1,128)S(1)}, u32[]{:S(2)}, u32[]{:S(2)}) async-start(f32[4,1,32]{2,1,0:T(1,128)} %broadcast_in_dim.52), calls=%async_computation.2 | async-start | bytes 4096 | tf_op jit(solution)/shard_map/all_to_all | solution.py:12
  7.6 8.4 %fusion.37 = f32[2,48,32,128]{3,2,1,0:T(8,128)S(1)} fusion(f32[2,48,32,128]{3,2,1,0:T(8,128)S(1)} %copy-done), kind=kOutput, calls=%fused_computation.105 | output fusion | flops 18481152 | bytes 3145728 | tf_op jit(solution)/shard_map/jit(cumsum)/reduce_window_sum | solution.py:123
  16.6 5.4 %all-to-all-start = ((f32[8,1,128]{2,1,0:T(1,128)}), f32[8,1,128]{2,1,0:T(1,128)S(1)}, u32[]{:S(2)}, u32[]{:S(2)}) async-start(f32[8,1,128]{2,1,0:T(1,128)} %broadcast_in_dim.47), calls=%async_computation | async-start | bytes 8192 | tf_op jit(solution)/shard_map/all_to_all | solution.py:12
  22.2 4.3 %all-to-all-done = f32[8,1,128]{2,1,0:T(1,128)S(1)} async-done(((f32[8,1,128]{2,1,0:T(1,128)}), f32[8,1,128]{2,1,0:T(1,128)S(1)}, u32[]{:S(2)}, u32[]{:S(2)}) %all-to-all-start) | async-done | bytes 4128 | tf_op jit(solution)/shard_map/all_to_all | solution.py:12
  27.3 8.2 %all-to-all-start.1 = ((f32[8,1,2,32,128]{4,3,2,1,0:T(8,128)}), f32[8,1,2,32,128]{4,3,2,1,0:T(8,128)S(1)}, u32[]{:S(2)}, u32[]{:S(2)}) async-start(f32[8,1,2,32,128]{4,3,2,1,0:T(8,128)} %broadcast_in_dim.49), calls=%async_computation.1 | async-start | bytes 524288 | tf_op jit(solution)/shard_map/all_to_all | solution.py:12
  35.7 10.2 %all-to-all-done.1 = f32[8,1,2,32,128]{4,3,2,1,0:T(8,128)S(1)} async-done(((f32[8,1,2,32,128]{4,3,2,1,0:T(8,128)}), f32[8,1,2,32,128]{4,3,2,1,0:T(8,128)S(1)}, u32[]{:S(2)}, u32[]{:S(2)}) %all-to-all-start.1) | async-done | bytes 262176 | tf_op jit(solution)/shard_map/all_to_all | solution.py:12
  49.1 3.6 %collective-permute-done.1 = f32[2,2,32,128]{3,2,1,0:T(8,128)S(1)} collective-permute-done((f32[2,2,32,128]{3,2,1,0:T(8,128)S(1)}, f32[2,2,32,128]{3,2,1,0:T(8,128)S(1)}, u32[]{:S(2)}, u32[]{:S(2)}) %collective-permute-start.1) | collective-permute-done | bytes 65568 | tf_op jit(solution)/shard_map/ppermute | solution.py:53
  52.9 6.7 %collective-permute-start.2 = (f32[2,52,2,128]{3,2,1,0:T(2,128)S(1)}, f32[2,52,2,128]{3,2,1,0:T(2,128)S(1)}, u32[]{:S(2)}, u32[]{:S(2)}) collective-permute-start(f32[2,52,2,128]{3,2,1,0:T(2,128)S(1)} %get-tuple-element.30), channel_id=1, source_target_pairs={{0,4},{4,8},{8,12},{12,16},{16,20},{20,24},{24,28},{1,5},{5,9},{9,... | collective-permute-start | bytes 319496 | tf_op jit(solution)/shard_map/ppermute | solution.py:50
  59.6 1.9 %collective-permute-start.3 = (f32[2,52,2,128]{3,2,1,0:T(2,128)S(1)}, f32[2,52,2,128]{3,2,1,0:T(2,128)S(1)}, u32[]{:S(2)}, u32[]{:S(2)}) collective-permute-start(f32[2,52,2,128]{3,2,1,0:T(2,128)S(1)} %get-tuple-element.31), channel_id=1, source_target_pairs={{4,0},{8,4},{12,8},{16,12},{20,16},{24,20},{28,24},{5,1},{9,5},{13... | collective-permute-start | bytes 319496 | tf_op jit(solution)/shard_map/ppermute | solution.py:53
  61.5 4.1 %collective-permute-done.3 = f32[2,52,2,128]{3,2,1,0:T(2,128)S(1)} collective-permute-done((f32[2,52,2,128]{3,2,1,0:T(2,128)S(1)}, f32[2,52,2,128]{3,2,1,0:T(2,128)S(1)}, u32[]{:S(2)}, u32[]{:S(2)}) %collective-permute-start.3) | collective-permute-done | bytes 106528 | tf_op jit(solution)/shard_map/ppermute | solution.py:53
  65.9 2.7 %fusion.36 = (f32[2,52,36,2]{3,2,1,0:T(8,128)}, f32[2,52,36,2]{3,2,1,0:T(8,128)}) fusion(f32[2,52,36,128]{3,2,1,0:T(8,128)S(1)} %pad_maximum_fusion.1), kind=kLoop, calls=%fused_computation.104 | loop fusion | bytes 119808 | tf_op jit(solution)/shard_map/slice | solution.py:51
  68.6 2.4 %copy.3 = f32[2,52,36,2]{1,3,2,0:T(2,128)S(1)} copy(f32[2,52,36,2]{3,2,1,0:T(8,128)} %get-tuple-element.25) | data formatting | bytes 59904 | tf_op jit(solution)/shard_map/slice | solution.py:51
  71.0 3.6 %collective-permute-start.4 = (f32[2,52,36,2]{1,3,2,0:T(2,128)S(1)}, f32[2,52,36,2]{1,3,2,0:T(2,128)S(1)}, u32[]{:S(2)}, u32[]{:S(2)}) collective-permute-start(f32[2,52,36,2]{1,3,2,0:T(2,128)S(1)} %copy.3), channel_id=1, source_target_pairs={{0,1},{1,2},{2,3},{4,5},{5,6},{6,7},{8,9},{9,10},{10,11},{12,13},{... | collective-permute-start | bytes 89864 | tf_op jit(solution)/shard_map/ppermute | solution.py:50
  74.7 2.4 %copy.4 = f32[2,52,36,2]{1,3,2,0:T(2,128)S(1)} copy(f32[2,52,36,2]{3,2,1,0:T(8,128)} %get-tuple-element.26) | data formatting | bytes 59904 | tf_op jit(solution)/shard_map/slice | solution.py:53
  80.1 2.2 %copy.5 = f32[2,52,36,2]{3,2,1,0:T(8,128)} copy(f32[2,52,36,2]{1,3,2,0:T(2,128)S(1)} %collective-permute-done.4) | data formatting | bytes 59904 | tf_op jit(solution)/shard_map/ppermute | solution.py:50
  82.3 2.2 %copy.6 = f32[2,52,36,2]{3,2,1,0:T(8,128)} copy(f32[2,52,36,2]{1,3,2,0:T(2,128)S(1)} %collective-permute-done.5) | data formatting | bytes 59904 | tf_op jit(solution)/shard_map/ppermute | solution.py:53
  84.5 6.1 %pad_maximum_fusion = f32[2,52,36,132]{3,2,1,0:T(8,128)S(1)} fusion(f32[2,52,36,2]{3,2,1,0:T(8,128)} %copy.6, f32[2,52,2,128]{3,2,1,0:T(2,128)S(1)} %collective-permute-done.3, f32[2,2,32,128]{3,2,1,0:T(8,128)S(1)} %collective-permute-done.1, f32[1,48,32,128]{3,2,1,0:T(8,128)S(1)} %get-tuple-element.35, f32[1,48,32,128]{3,2,1,0:T(8,128)S(1)} %get-tuple-element.34, ...), kind=kLoop, calls=%fused_computation.4 | loop fusion | flops 3459456 | bytes 3953664 | tf_op jit(solution)/shard_map/concatenate | solution.py:54
  91.8 4.5 %subtract_bitcast_fusion.2 = (f32[1,50,34,130]{3,2,1,0:T(8,128)S(1)}, f32[50,34,130]{2,1,0:T(8,128)S(1)}, f32[50,34,130]{2,1,0:T(8,128)S(1)}, f32[50,34,130]{2,1,0:T(8,128)S(1)}) fusion(f32[51,35,131]{2,1,0:T(8,128)S(1)} %get-tuple-element.23, f32[51,35,131]{2,1,0:T(8,128)S(1)} %get-tuple-element.24, f32[51,35,131]{2,1,0:T(8,128)S(1)} %get-tuple-element.22), kind=kLoop, calls=%fused_computation.37 | loop fusion | flops 6409000 | bytes 11492000 | tf_op jit(solution)/shard_map/stack | solution.py:100
  96.3 2.8 %subtract_bitcast_fusion.1 = (f32[1,50,34,130]{3,2,1,0:T(8,128)S(1)}, f32[1,50,34,130]{3,2,1,0:T(8,128)S(1)}) fusion(f32[50,34,130]{2,1,0:T(8,128)S(1)} %get-tuple-element.12, f32[50,34,130]{2,1,0:T(8,128)S(1)} %get-tuple-element.11, f32[50,34,130]{2,1,0:T(8,128)S(1)} %get-tuple-element.10, f32[51,35,131]{2,1,0:T(8,128)S(1)} %get-tuple-element.23, ...), kind=kLoop, calls=%fused_computation.35 | loop fusion | flops 5304000 | bytes 7072000 | tf_op jit(solution)/shard_map/stack | solution.py:100
  101.1 2.2 %copy-done.2 = f32[3,50,34,130]{3,2,1,0:T(8,128)} copy-done((f32[3,50,34,130]{3,2,1,0:T(8,128)}, f32[3,50,34,130]{3,2,1,0:T(8,128)S(1)}, u32[]{:S(2)}) %copy-start.2) | copy-done | bytes 2652024
  103.3 3.4 %fusion.19 = (f32[49,33,129]{2,1,0:T(8,128)S(1)}, f32[49,33,129]{2,1,0:T(8,128)}, f32[49,33,129]{2,1,0:T(8,128)}) fusion(f32[50,34,130]{2,1,0:T(8,128)S(1)} %get-tuple-element.17, f32[50,34,130]{2,1,0:T(8,128)S(1)} %get-tuple-element.19, f32[50,34,130]{2,1,0:T(8,128)S(1)} %get-tuple-element.18), kind=kLoop, calls=%fused_computation.52 | loop fusion | flops 2503116 | bytes 10012464 | tf_op jit(solution)/shard_map/div | solution.py:81
  106.7 5.9 %subtract_bitcast_fusion.5 = (f32[1,48,32,128]{3,2,1,0:T(8,128)S(1)}, f32[48,32,128]{2,1,0:T(8,128)S(1)}, f32[48,32,128]{2,1,0:T(8,128)S(1)}, f32[48,32,128]{2,1,0:T(8,128)S(1)}) fusion(f32[49,33,129]{2,1,0:T(8,128)} %get-tuple-element.28, f32[49,33,129]{2,1,0:T(8,128)} %get-tuple-element.29, f32[49,33,129]{2,1,0:T(8,128)S(1)} %get-tuple-element.27), kind=kLoop, calls=%fused_computation.74 | loop fusion | flops 5701632 | bytes 10223616 | tf_op jit(solution)/shard_map/stack | solution.py:100
  112.6 3.4 %subtract_bitcast_fusion.4 = (f32[1,48,32,128]{3,2,1,0:T(8,128)S(1)}, f32[1,48,32,128]{3,2,1,0:T(8,128)S(1)}) fusion(f32[48,32,128]{2,1,0:T(8,128)S(1)} %get-tuple-element.8, f32[48,32,128]{2,1,0:T(8,128)S(1)} %get-tuple-element.7, f32[48,32,128]{2,1,0:T(8,128)S(1)} %get-tuple-element.6, f32[49,33,129]{2,1,0:T(8,128)} %get-tuple-element.28, ...), kind=kLoop, calls=%fused_computation.72 | loop fusion | flops 4718592 | bytes 6291456 | tf_op jit(solution)/shard_map/stack | solution.py:100
  116.0 5.0 %slice_add_fusion = f32[3,48,32,128]{3,2,1,0:T(8,128)} fusion(f32[3,50,34,130]{3,2,1,0:T(8,128)} %copy-done.2, f32[1,48,32,128]{3,2,1,0:T(8,128)S(1)} %get-tuple-element.16, f32[1,48,32,128]{3,2,1,0:T(8,128)S(1)} %get-tuple-element.15, f32[1,48,32,128]{3,2,1,0:T(8,128)S(1)} %get-tuple-element.5), kind=kLoop, calls=%fused_computation.5 | loop fusion | flops 2359296 | bytes 7077888 | tf_op jit(solution)/shard_map/add | solution.py:100
  (56 shorter events, 14.3 us)
Async XLA Ops:
  0.0 7.5 %copy-start = (f32[2,48,32,128]{3,2,1,0:T(8,128)S(1)}, f32[2,48,32,128]{3,2,1,0:T(8,128)}, u32[]{:S(2)}) copy-start(f32[2,48,32,128]{3,2,1,0:T(8,128)} %param.2) | copy-start | bytes 4718596
  1.9 14.1 %all-to-all-start.2 = ((f32[4,1,32]{2,1,0:T(1,128)}), f32[4,1,32]{2,1,0:T(1,128)S(1)}, u32[]{:S(2)}, u32[]{:S(2)}) async-start(f32[4,1,32]{2,1,0:T(1,128)} %broadcast_in_dim.52), calls=%async_computation.2 | async-start | bytes 4096 | tf_op jit(solution)/shard_map/all_to_all | solution.py:12
  16.6 9.9 %all-to-all-start = ((f32[8,1,128]{2,1,0:T(1,128)}), f32[8,1,128]{2,1,0:T(1,128)S(1)}, u32[]{:S(2)}, u32[]{:S(2)}) async-start(f32[8,1,128]{2,1,0:T(1,128)} %broadcast_in_dim.47), calls=%async_computation | async-start | bytes 8192 | tf_op jit(solution)/shard_map/all_to_all | solution.py:12
  27.3 18.6 %all-to-all-start.1 = ((f32[8,1,2,32,128]{4,3,2,1,0:T(8,128)}), f32[8,1,2,32,128]{4,3,2,1,0:T(8,128)S(1)}, u32[]{:S(2)}, u32[]{:S(2)}) async-start(f32[8,1,2,32,128]{4,3,2,1,0:T(8,128)} %broadcast_in_dim.49), calls=%async_computation.1 | async-start | bytes 524288 | tf_op jit(solution)/shard_map/all_to_all | solution.py:12
  46.4 2.8 %collective-permute-start = (f32[2,2,32,128]{3,2,1,0:T(8,128)S(1)}, f32[2,2,32,128]{3,2,1,0:T(8,128)S(1)}, u32[]{:S(2)}, u32[]{:S(2)}) collective-permute-start(f32[2,2,32,128]{3,2,1,0:T(8,128)S(1)} %get-tuple-element.32), channel_id=1, source_target_pairs={{0,32},{32,64},{64,96},{96,128},{128,160},{160,192},{192,224},{1,3... | collective-permute-start | bytes 196616 | tf_op jit(solution)/shard_map/ppermute | solution.py:50
  47.8 5.0 %collective-permute-start.1 = (f32[2,2,32,128]{3,2,1,0:T(8,128)S(1)}, f32[2,2,32,128]{3,2,1,0:T(8,128)S(1)}, u32[]{:S(2)}, u32[]{:S(2)}) collective-permute-start(f32[2,2,32,128]{3,2,1,0:T(8,128)S(1)} %get-tuple-element.33), channel_id=1, source_target_pairs={{32,0},{64,32},{96,64},{128,96},{160,128},{192,160},{224,192},{33,... | collective-permute-start | bytes 196616 | tf_op jit(solution)/shard_map/ppermute | solution.py:53
  52.9 8.7 %collective-permute-start.2 = (f32[2,52,2,128]{3,2,1,0:T(2,128)S(1)}, f32[2,52,2,128]{3,2,1,0:T(2,128)S(1)}, u32[]{:S(2)}, u32[]{:S(2)}) collective-permute-start(f32[2,52,2,128]{3,2,1,0:T(2,128)S(1)} %get-tuple-element.30), channel_id=1, source_target_pairs={{0,4},{4,8},{8,12},{12,16},{16,20},{20,24},{24,28},{1,5},{5,9},{9,... | collective-permute-start | bytes 319496 | tf_op jit(solution)/shard_map/ppermute | solution.py:50
  59.6 6.0 %collective-permute-start.3 = (f32[2,52,2,128]{3,2,1,0:T(2,128)S(1)}, f32[2,52,2,128]{3,2,1,0:T(2,128)S(1)}, u32[]{:S(2)}, u32[]{:S(2)}) collective-permute-start(f32[2,52,2,128]{3,2,1,0:T(2,128)S(1)} %get-tuple-element.31), channel_id=1, source_target_pairs={{4,0},{8,4},{12,8},{16,12},{20,16},{24,20},{28,24},{5,1},{9,5},{13... | collective-permute-start | bytes 319496 | tf_op jit(solution)/shard_map/ppermute | solution.py:53
  71.0 9.1 %collective-permute-start.4 = (f32[2,52,36,2]{1,3,2,0:T(2,128)S(1)}, f32[2,52,36,2]{1,3,2,0:T(2,128)S(1)}, u32[]{:S(2)}, u32[]{:S(2)}) collective-permute-start(f32[2,52,36,2]{1,3,2,0:T(2,128)S(1)} %copy.3), channel_id=1, source_target_pairs={{0,1},{1,2},{2,3},{4,5},{5,6},{6,7},{8,9},{9,10},{10,11},{12,13},{... | collective-permute-start | bytes 89864 | tf_op jit(solution)/shard_map/ppermute | solution.py:50
  77.0 5.3 %collective-permute-start.5 = (f32[2,52,36,2]{1,3,2,0:T(2,128)S(1)}, f32[2,52,36,2]{1,3,2,0:T(2,128)S(1)}, u32[]{:S(2)}, u32[]{:S(2)}) collective-permute-start(f32[2,52,36,2]{1,3,2,0:T(2,128)S(1)} %copy.4), channel_id=1, source_target_pairs={{1,0},{2,1},{3,2},{5,4},{6,5},{7,6},{9,8},{10,9},{11,10},{13,12},{... | collective-permute-start | bytes 89864 | tf_op jit(solution)/shard_map/ppermute | solution.py:53
  96.3 2.8 %copy-start.3 = (f32[50,34,130]{2,1,0:T(8,128)S(1)}, f32[50,34,130]{2,1,0:T(8,128)}, u32[]{:S(2)}) copy-start(f32[50,34,130]{2,1,0:T(8,128)} %broadcast_multiply_fusion) | copy-start | bytes 2652004
  100.7 2.6 %copy-start.2 = (f32[3,50,34,130]{3,2,1,0:T(8,128)}, f32[3,50,34,130]{3,2,1,0:T(8,128)S(1)}, u32[]{:S(2)}) copy-start(f32[3,50,34,130]{3,2,1,0:T(8,128)S(1)} %fusion.1) | copy-start | bytes 7956004
  116.0 5.0 %copy-start.1 = (f32[2,48,32,128]{3,2,1,0:T(8,128)S(1)}, f32[2,48,32,128]{3,2,1,0:T(8,128)}, u32[]{:S(2)}) copy-start(f32[2,48,32,128]{3,2,1,0:T(8,128)} %param.2) | copy-start | bytes 4718596
where the time goes:
time: 122 us; the launch traced here: 121 us
  other arithmetic  46.6 us (38%)
  starting transfers between devices  34.9 us (29%)
  waiting for transfers between devices  22.3 us (18%)
  local copies, waits for them, and re-layouts  16.9 us (14%)
    all_to_all x3, starting transfers between devices, from_everyone(): return lax.all_to_all(copies, axis, split_axis=0, concat_axis=0, tiled=True)  18.4 us
    another operation x4, other arithmetic, advance(): return inner + friction * jnp.stack([drive_x, drive_y, drive_z])  16.6 us
    all_to_all x3, waiting for transfers between devices, from_everyone(): return lax.all_to_all(copies, axis, split_axis=0, concat_axis=0, tiled=True)  14.5 us
    ppermute x3, starting transfers between devices, with_halo(): lax.ppermute(lax.slice_in_dim(block, block.shape[dim] - width, None, axis...  11.7 us
    another operation x1, other arithmetic, local(): vertical = jnp.cumsum(side_field, axis=1)  8.39 us
    ppermute x3, waiting for transfers between devices, with_halo(): lax.ppermute(lax.slice_in_dim(block, 0, width, axis=dim), axis, backward)  7.7 us
    concatenate x2, other arithmetic, with_halo(): block = jnp.concatenate([low, block, high], axis=dim)  6.41 us
    slice x2, local copies, waits for them, and re-layouts, with_halo(): lax.slice_in_dim(block, block.shape[dim] - width, None, axis=dim)  5.06 us
  transfers between devices with their start and end apart: 9, of which 4 were waited for; matrix products, arithmetic and copies ran while one was open for 13% of the time, Pallas kernels for 0%

commit v1 on v0

v1 whole, which is shorter than its diff:
```python
import functools

import jax
import jax.numpy as jnp
from jax import lax
from jax.experimental import pallas as pl
from jax.experimental.pallas import tpu as pltpu
from jax.sharding import PartitionSpec as P

spacing = 0.0625
friction = 0.004
MESH = pl.DeviceIdType.MESH

NZ_DEV, NY_DEV, NX_DEV = 8, 8, 4
CZ, CY, CX = 48, 32, 128
EZ = CZ + 3
EY = CY + 8
LEVEL = EZ * CY
UP, DOWN = 4, 3


def lanes(shape):
    return lax.broadcasted_iota(jnp.int32, shape, len(shape) - 1)


def rows(shape):
    return lax.broadcasted_iota(jnp.int32, shape, len(shape) - 2)


def comm_kernel(
    side_hbm,
    mag_ref,
    ext_out,
    zh_out,
    q_out,
    e_out,
    side_v,
    t_v,
    ring_up,
    ring_dn,
    ys_lo,
    ys_hi,
    yr_lo,
    yr_hi,
    cs_lo,
    cs_hi,
    cr_lo,
    cr_hi,
    w_hi,
    w_lo,
    wn_hi,
    wn_lo,
    mc_s,
    mr_s,
    mc_r,
    mr_r,
    q_v,
    qt_lo,
    qt_hi,
    qy_lo,
    qy_hi,
    qx_lo,
    qx_hi,
    qd,
    load_sem,
    s_up,
    r_up,
    s_dn,
    r_dn,
    s_z,
    r_z,
    s_y,
    r_y,
    s_c,
    r_c,
    s_w,
    r_w,
    s_mc,
    r_mc,
    s_mr,
    r_mr,
    s_q,
    r_q,
):
    gz, gy, gx = lax.axis_index("gz"), lax.axis_index("gy"), lax.axis_index("gx")

    def at(dz=0, dy=0, dx=0):
        where = {}
        if dz:
            where["gz"] = lax.rem(gz + dz + NZ_DEV, NZ_DEV)
        if dy:
            where["gy"] = lax.rem(gy + dy + NY_DEV, NY_DEV)
        if dx:
            where["gx"] = lax.rem(gx + dx + NX_DEV, NX_DEV)
        return where

    loads = [
        pltpu.make_async_copy(
            side_hbm.at[pl.ds(c * CZ * CY, CZ * CY)],
            side_v.at[pl.ds(c * LEVEL + CY, CZ * CY)],
            load_sem.at[c],
        )
        for c in range(2)
    ]
    for load in loads:
        load.start()

    barrier = pltpu.get_barrier_semaphore()
    peers = (
        [at(dz=1), at(dz=-1)]
        + [at(dy=d) for d in range(1, NY_DEV)]
        + [at(dx=d) for d in range(1, NX_DEV)]
        + [at(dy=a, dx=b) for a in (1, -1) for b in (1, -1)]
    )
    for peer in peers:
        pl.semaphore_signal(barrier, inc=1, device_id=peer, device_id_type=MESH)

    def send(src, dst, ssem, rsem, where):
        return pltpu.make_async_remote_copy(
            src_ref=src,
            dst_ref=dst,
            send_sem=ssem,
            recv_sem=rsem,
            device_id=where,
            device_id_type=MESH,
        )

    mag = mag_ref[...]
    mc_s[...] = jnp.broadcast_to(jnp.sum(mag, axis=0, keepdims=True), (8, CX))
    mr_s[...] = jnp.broadcast_to(jnp.sum(mag, axis=1, keepdims=True), (CY, CX))
    ext_out[...] = jnp.zeros_like(ext_out)

    for c in range(2):
        loads[c].wait()

        def add(z, total, c=c):
            return total + side_v[pl.ds(c * LEVEL + (z + 1) * CY, CY), :]

        t_v[pl.ds(c * CY, CY), :] = lax.fori_loop(
            0, CZ, add, jnp.zeros((CY, CX), jnp.float32), unroll=8
        )
    pl.semaphore_wait(barrier, len(peers))

    def up(s, c):
        src = t_v.at[pl.ds(c * CY, CY)] if s == 0 else ring_up.at[s - 1, pl.ds(c * CY, CY)]
        return send(
            src, ring_up.at[s, pl.ds(c * CY, CY)], s_up.at[s, c], r_up.at[s, c], at(dz=1)
        )

    def down(s, c):
        src = t_v.at[pl.ds(c * CY, CY)] if s == 0 else ring_dn.at[s - 1, pl.ds(c * CY, CY)]
        return send(
            src, ring_dn.at[s, pl.ds(c * CY, CY)], s_dn.at[s, c], r_dn.at[s, c], at(dz=-1)
        )

    ups = [[up(s, c) for c in range(2)] for s in range(UP)]
    downs = [[down(s, c) for c in range(2)] for s in range(DOWN)]
    for c in range(2):
        ups[0][c].start()
        downs[0][c].start()

    sums = [
        send(mc_s, mc_r.at[pl.ds(8 * (d - 1), 8)], s_mc.at[d - 1], r_mc.at[d - 1], at(dy=d))
        for d in range(1, NY_DEV)
    ] + [
        send(mr_s, mr_r.at[pl.ds(CY * (d - 1), CY)], s_mr.at[d - 1], r_mr.at[d - 1], at(dx=d))
        for d in range(1, NX_DEV)
    ]
    for one in sums:
        one.start()

    layers = []
    for c in range(2):
        layers.append(
            send(
                side_hbm.at[pl.ds(c * CZ * CY + (CZ - 1) * CY, CY)],
                side_v.at[pl.ds(c * LEVEL, CY)],
                s_z.at[0, c],
                r_z.at[0, c],
                at(dz=1),
            )
        )
        layers.append(
            send(
                side_hbm.at[pl.ds(c * CZ * CY, 2 * CY)],
                side_v.at[pl.ds(c * LEVEL + (CZ + 1) * CY, 2 * CY)],
                s_z.at[1, c],
                r_z.at[1, c],
                at(dz=-1),
            )
        )
    for one in layers:
        one.start()

    for c in range(2):
        for k in range(2):
            here = pl.ds((2 * c + k) * CZ, CZ)
            ys_lo[here, :] = side_v[pl.ds(c * LEVEL + CY + k, CZ, stride=CY), :]
            ys_hi[here, :] = side_v[pl.ds(c * LEVEL + CY + CY - 2 + k, CZ, stride=CY), :]
    faces = [
        send(ys_lo, yr_hi, s_y.at[0], r_y.at[0], at(dy=-1)),
        send(ys_hi, yr_lo, s_y.at[1], r_y.at[1], at(dy=1)),
    ]
    for one in faces:
        one.start()

    def pass_on(s):
        for c in range(2):
            ups[s][c].wait_recv()
            if s + 1 < UP:
                ups[s + 1][c].start()
            if s < DOWN:
                downs[s][c].wait_recv()
                if s + 1 < DOWN:
                    downs[s + 1][c].start()

    pass_on(0)

    for one in layers:
        one.wait_recv()
    for c in range(2):
        for i, level in enumerate((0, CZ + 1, CZ + 2)):
            first = c * LEVEL + level * CY
            to = (c * 3 + i) * 2
            cs_lo[pl.ds(to, 2), :] = side_v[pl.ds(first, 2), :]
            cs_hi[pl.ds(to, 2), :] = side_v[pl.ds(first + CY - 2, 2), :]
            zh_out[pl.ds((c * 3 + i) * CY, CY), :] = side_v[pl.ds(first, CY), :]
    cs_lo[pl.ds(12, 4), :] = jnp.zeros((4, CX), jnp.float32)
    cs_hi[pl.ds(12, 4), :] = jnp.zeros((4, CX), jnp.float32)
    corners = [
        send(cs_lo, cr_hi, s_c.at[0], r_c.at[0], at(dy=-1)),
        send(cs_hi, cr_lo, s_c.at[1], r_c.at[1], at(dy=1)),
    ]
    for one in corners:
        one.start()

    has_ylo = (gy > 0).astype(jnp.float32)
    has_yhi = (gy < NY_DEV - 1).astype(jnp.float32)
    has_xlo = (gx > 0).astype(jnp.float32)
    has_xhi = (gx < NX_DEV - 1).astype(jnp.float32)

    for one in faces:
        one.wait_recv()
    for c in range(2):
        for k in range(2):
            here = pl.ds((2 * c + k) * CZ, CZ)
            ext_out[pl.ds((c * EZ + 1) * 8 + k, CZ, stride=8), :] = yr_hi[here, :] * has_yhi
            ext_out[pl.ds((c * EZ + 1) * 8 + 6 + k, CZ, stride=8), :] = yr_lo[here, :] * has_ylo

    pass_on(1)

    for one in corners:
        one.wait_recv()
    for c in range(2):
        for i, level in enumerate((0, CZ + 1, CZ + 2)):
            first = (c * EZ + level) * 8
            of = (c * 3 + i) * 2
            ext_out[pl.ds(first, 2), :] = cr_hi[pl.ds(of, 2), :] * has_yhi
            ext_out[pl.ds(first + 6, 2), :] = cr_lo[pl.ds(of, 2), :] * has_ylo

    lane = lanes((EY, CX))

    def raw(c, level):
        return jnp.concatenate(
            [
                side_v[pl.ds(pl.multiple_of(c * LEVEL + level * CY, 8), CY), :],
                ext_out[pl.ds(pl.multiple_of((c * EZ + level) * 8, 8), 8), :],
            ],
            axis=0,
        )

    def place(zi, running, packed):
        first = 2 * zi
        out = []
        for c in range(2):
            turned = pltpu.roll(running[c], first + 2, 1)
            hi, lo = packed[2 * c], packed[2 * c + 1]
            out.append(jnp.where((lane == first) | (lane == first + 1), turned, hi))
            out.append(jnp.where((lane == first + 2) | (lane == first + 3), turned, lo))
        return tuple(out)

    nothing = jnp.zeros((EY, CX), jnp.float32)
    running = tuple(-raw(c, 0) for c in range(2))
    packed = place(0, running, (nothing,) * 4)

    def pack(zi, carry):
        running, packed = carry
        running = tuple(running[c] + raw(c, zi - 1) for c in range(2))
        return running, place(zi, running, packed)

    _, packed = lax.fori_loop(1, EZ + 1, pack, (running, packed))
    for c in range(2):
        w_hi[pl.ds(c * EY, EY), :] = packed[2 * c]
        w_lo[pl.ds(c * EY, EY), :] = packed[2 * c + 1]
    columns = [
        send(w_hi, wn_lo, s_w.at[0], r_w.at[0], at(dx=1)),
        send(w_lo, wn_hi, s_w.at[1], r_w.at[1], at(dx=-1)),
    ]
    for one in columns:
        one.start()

    for one in sums:
        one.wait_recv()
    col = mag
    row_of = rows((CY, CX))
    for k in (1, 2, 4, 8, 16):
        col = col + jnp.where(row_of >= k, pltpu.roll(col, k, 0), 0.0)
    lin = mag
    lane_of = lanes((CY, CX))
    for k in (1, 2, 4, 8, 16, 32, 64):
        lin = lin + jnp.where(lane_of >= k, pltpu.roll(lin, k, 1), 0.0)
    for d in range(1, NY_DEV):
        part = mc_r[pl.ds(8 * (d - 1), 1), :]
        col = col + jnp.where(d <= gy, part, 0.0)
    for d in range(1, NX_DEV):
        part = mr_r[pl.ds(CY * (d - 1), CY), :]
        lin = lin + jnp.where(d <= gx, part, 0.0)
    base = (-0.5 * spacing * col, 0.5 * spacing * lin)

    pass_on(2)
    below = [jnp.zeros((CY, CX), jnp.float32) for _ in range(2)]
    for c in range(2):
        for s in range(3):
            part = ring_up[s, pl.ds(c * CY, CY), :]
            below[c] = below[c] + jnp.where(gz - (s + 1) >= 0, part, 0.0)
            part = ring_dn[s, pl.ds(c * CY, CY), :]
            below[c] = below[c] + jnp.where(gz + (s + 1) >= NZ_DEV, part, 0.0)

    for one in columns:
        one.wait_recv()

    pass_on(3)
    for c in range(2):
        part = ring_up[3, pl.ds(c * CY, CY), :]
        below[c] = below[c] + jnp.where(gz - 4 >= 0, part, 0.0)
    q = (base[0] + spacing * below[1], base[1] - spacing * below[0])
    for c in range(2):
        q_v[pl.ds(c * CY, CY), :] = q[c]
        qt_lo[pl.ds(c * 8, 8), :] = q[c][:8]
        qt_hi[pl.ds(c * 8, 8), :] = q[c][CY - 8 :]
    planes = [
        send(q_v, qx_lo, s_q.at[0], r_q.at[0], at(dx=1)),
        send(q_v, qx_hi, s_q.at[1], r_q.at[1], at(dx=-1)),
        send(qt_lo, qy_hi, s_q.at[2], r_q.at[2], at(dy=-1)),
        send(qt_hi, qy_lo, s_q.at[3], r_q.at[3], at(dy=1)),
        send(qt_lo, qd.at[0], s_q.at[4], r_q.at[4], at(dy=-1, dx=1)),
        send(qt_lo, qd.at[1], s_q.at[5], r_q.at[5], at(dy=-1, dx=-1)),
        send(qt_hi, qd.at[2], s_q.at[6], r_q.at[6], at(dy=1, dx=1)),
        send(qt_hi, qd.at[3], s_q.at[7], r_q.at[7], at(dy=1, dx=-1)),
    ]
    for one in planes:
        one.start()
    for one in planes:
        one.wait_recv()

    row8 = rows((8, CX))

    def fifth(from_hi, from_lo):
        return jnp.where(
            row8 < 2, from_hi * has_yhi, jnp.where(row8 >= 6, from_lo * has_ylo, 0.0)
        )

    def plane(main, from_hi, from_lo, c):
        tile = fifth(from_hi[pl.ds(c * 8, 8), :], from_lo[pl.ds(c * 8, 8), :])
        return jnp.concatenate([main, tile], axis=0)

    even = lane % 2 == 0
    level_ok = ((lane >= 4) | (gz > 0)) & ((lane < 2 * (CZ + 2)) | (gz < NZ_DEV - 1))
    for c in range(2):
        own = plane(q[c], qy_hi, qy_lo, c)
        low = plane(qx_lo[pl.ds(c * CY, CY), :], qd.at[0], qd.at[2], c) * has_xlo
        high = plane(qx_hi[pl.ds(c * CY, CY), :], qd.at[1], qd.at[3], c) * has_xhi
        q_out[pl.ds(c * EY, EY), :] = own

        o, sign = (1, spacing) if c == 0 else (0, -spacing)
        there = pl.ds(o * EY, EY)
        hi, lo = w_hi[there, :], w_lo[there, :]
        hin, lon = wn_hi[there, :] * has_xhi, wn_lo[there, :] * has_xlo

        def spread(x, i):
            return jnp.broadcast_to(x[:, i : i + 1], (EY, CX))

        parts = (
            (spread(own, 126), spread(low, 126), hi, pltpu.roll(lon, 1, 1)),
            (spread(own, 127), spread(low, 127), pltpu.roll(hi, CX - 1, 1), lon),
            (spread(high, 0), spread(own, 0), pltpu.roll(hin, CX - 2, 1), pltpu.roll(lo, CX - 1, 1)),
            (spread(high, 1), spread(own, 1), pltpu.roll(hin, CX - 3, 1), pltpu.roll(lo, CX - 2, 1)),
        )
        for m, (q_hi, q_lo, l_hi, l_lo) in enumerate(parts):
            value = jnp.where(even, q_hi, q_lo) + sign * jnp.where(even, l_hi, l_lo)
            e_out[pl.ds((m * 2 + c) * EY, EY), :] = jnp.where(level_ok, value, 0.0)

    for group in ups + downs:
        for one in group:
            one.wait_send()
    for one in sums + layers + faces + corners + columns + planes:
        one.wait_send()


def turn(x, shift, axis):
    return pltpu.roll(x, shift % x.shape[axis], axis)


def fields(a, zp, yp, xp, first):
    ax, ay = a[0], a[1]
    if first:
        bx = ay - zp[1]
        by = zp[0] - ax
    else:
        bx = (yp[2] - a[2]) - (zp[1] - ay)
        by = (zp[0] - ax) - (xp[2] - a[2])
    bz = (xp[1] - ay) - (yp[0] - ax)
    return bx, by, bz


def drive(b, zm, ym, xm):
    bx, by, bz = b
    jx = (bz - ym[2]) - (by - zm[1])
    jy = (bx - zm[0]) - (bz - xm[2])
    jz = (by - xm[1]) - (bx - ym[0])
    square = bx * bx + by * by + bz * bz
    scale = (friction / spacing**2) / (square + spacing**2)
    along = (jx * bx + jy * by + jz * bz) * scale
    across = square * scale
    return (along * bx - across * jx, along * by - across * jy, along * bz - across * jz)


def step_kernel(
    side_hbm,
    ext_ref,
    zh_ref,
    q_ref,
    e_ref,
    out_hbm,
    side_v,
    a1m,
    a1e,
    out_v,
    load_sem,
    store_sem,
):
    gz, gy, gx = lax.axis_index("gz"), lax.axis_index("gy"), lax.axis_index("gx")
    loads = [
        pltpu.make_async_copy(
            side_hbm.at[pl.ds(c * CZ * CY, CZ * CY)],
            side_v.at[pl.ds(c * LEVEL + CY, CZ * CY)],
            load_sem.at[c],
        )
        for c in range(2)
    ]
    for load in loads:
        load.start()
    for c in range(2):
        for i, level in enumerate((0, CZ + 1, CZ + 2)):
            side_v[pl.ds(c * LEVEL + level * CY, CY), :] = zh_ref[pl.ds((c * 3 + i) * CY, CY), :]

    shape = (EY, CX)
    lane, row = lanes(shape), rows(shape)
    even = lane % 2 == 0
    row_ok = ((row < CY) | (row >= CY + 2) | (gy < NY_DEV - 1)) & (
        (row < CY + 2) | (gy > 0)
    )

    ea = [[e_ref[pl.ds((m * 2 + c) * EY, EY), :] for c in range(2)] for m in range(4)]
    eb = []
    for m in range(3):
        up_y = (turn(ea[m][0], -1, 0),)
        up_z = tuple(turn(x, -2, 1) for x in ea[m])
        eb.append(fields(ea[m], up_z, up_y, ea[m + 1], True))
    ea1 = []
    for m in (1, 2):
        down_z = tuple(turn(x, 2, 1) for x in eb[m])
        down_y = tuple(turn(x, 1, 0) for x in eb[m])
        d = drive(eb[m], down_z, down_y, eb[m - 1])
        outside = (lane % 2 == 1) & (gx == 0) if m == 1 else (lane % 2 == 0) & (gx == NX_DEV - 1)
        ok = (
            row_ok
            & jnp.logical_not(outside)
            & ((lane >= 4) | (gz > 0))
            & ((lane < 2 * (CZ + 2)) | (gz < NZ_DEV - 1))
        )
        a = (ea[m][0] + d[0], ea[m][1] + d[1], d[2])
        ea1.append(tuple(jnp.where(ok, x, 0.0) for x in a))
    u1 = jnp.where(even, ea[2][1], eb[1][2])
    u2 = eb[1][1]
    near = ea1[0]
    eb1 = fields(
        near,
        tuple(turn(x, -2, 1) for x in near),
        tuple(turn(x, -1, 0) for x in near),
        ea1[1],
        False,
    )
    v1 = jnp.where(even, ea1[1][1], eb1[2])
    v2 = jnp.where(even, ea1[1][2], eb1[1])

    def raw(c, level):
        return jnp.concatenate(
            [
                side_v[pl.ds(pl.multiple_of(c * LEVEL + level * CY, 8), CY), :],
                ext_ref[pl.ds(pl.multiple_of((c * EZ + level) * 8, 8), 8), :],
            ],
            axis=0,
        )

    in_lo = (gz > 0).astype(jnp.float32)
    in_hi = (gz < NZ_DEV - 1).astype(jnp.float32)
    first_lane, last_lane = lane == 0, lane == CX - 1
    tile_row = rows((8, CX))
    tile_ok = ((tile_row >= 2) | (gy < NY_DEV - 1)) & ((tile_row < 2) | (gy > 0))

    def grow(a, level):
        return (a[0] + spacing * raw(1, level), a[1] - spacing * raw(0, level))

    def field_at(a, a_up, u):
        xp = (None, jnp.where(last_lane, u[0], turn(a[1], -1, 1)))
        return fields(a, a_up, (turn(a[0], -1, 0),), xp, True)

    def first_step(a, b, before, u, store, ok=None):
        xm = (
            None,
            jnp.where(first_lane, u[1], turn(b[1], 1, 1)),
            jnp.where(first_lane, u[0], turn(b[2], 1, 1)),
        )
        ym = (turn(b[0], 1, 0), None, turn(b[2], 1, 0))
        d = drive(b, before, ym, xm)
        new = (a[0] + d[0], a[1] + d[1], d[2])
        for c in range(3):
            x = new[c] if ok is None else new[c] * ok
            a1m[pl.ds(pl.multiple_of((c * (CZ + 2) + store) * CY, 8), CY), :] = x[:CY]
            a1e[pl.ds(pl.multiple_of((c * (CZ + 2) + store) * 8, 8), 8), :] = jnp.where(
                tile_ok, x[CY:], 0.0
            )

    def advance_u(u):
        return tuple(turn(x, -2, 1) for x in u)

    for load in loads:
        load.wait()
    q = tuple(q_ref[pl.ds(c * EY, EY), :] for c in range(2))
    bottom = tuple(x * in_lo for x in q)
    lowest = (
        (q[0] - spacing * raw(1, 0)) * in_lo,
        (q[1] + spacing * raw(0, 0)) * in_lo,
    )
    u = tuple(turn(x, CX - 1, 1) for x in (u1, u2))
    b = field_at(lowest, bottom, u)
    u = advance_u(u)
    a = grow(q, 1)
    before = (b[0], b[1])
    b = field_at(bottom, a, u)
    first_step(bottom, b, before, u, 0, in_lo)
    u = advance_u(u)

    def level_one(z, carry):
        a, before, u = carry
        a_up = grow(a, z + 2)
        b = field_at(a, a_up, u)
        first_step(a, b, before, u, z + 1)
        return a_up, (b[0], b[1]), advance_u(u)

    a, before, u = lax.fori_loop(0, CZ - 1, level_one, (a, (b[0], b[1]), u))
    top = tuple(x * in_hi for x in grow(a, CZ + 1))
    b = field_at(a, top, u)
    first_step(a, b, before, u, CZ)
    u = advance_u(u)
    above = tuple(x * in_hi for x in grow(top, CZ + 2))
    before = (b[0], b[1])
    b = field_at(top, above, u)
    first_step(top, b, before, u, CZ + 1, in_hi)

    def new_at(store):
        return tuple(
            jnp.concatenate(
                [
                    a1m[pl.ds(pl.multiple_of((c * (CZ + 2) + store) * CY, 8), CY), :],
                    a1e[pl.ds(pl.multiple_of((c * (CZ + 2) + store) * 8, 8), 8), :],
                ],
                axis=0,
            )
            for c in range(3)
        )

    def second_field(a, a_up, v):
        yp = (turn(a[0], -1, 0), None, turn(a[2], -1, 0))
        xp = (
            None,
            jnp.where(last_lane, v[0], turn(a[1], -1, 1)),
            jnp.where(last_lane, v[1], turn(a[2], -1, 1)),
        )
        return fields(a, a_up, yp, xp, False)

    first_main, main = first_lane[:CY], slice(0, CY)

    def level_two(z, carry):
        a, before, v = carry
        a_up = new_at(z + 2)
        b = second_field(a, a_up, v)
        ym = (turn(b[0], 1, 0)[main], None, turn(b[2], 1, 0)[main])
        own = tuple(x[main] for x in b)
        xm = (
            None,
            jnp.where(first_main, v[1][main], turn(own[1], 1, 1)),
            jnp.where(first_main, v[0][main], turn(own[2], 1, 1)),
        )
        d = drive(own, before, ym, xm)
        for c in range(3):
            out_v[pl.ds(pl.multiple_of((c * CZ + z) * CY, 8), CY), :] = a[c][main] + d[c]
        return a_up, (own[0], own[1]), advance_u(v)

    v = tuple(turn(x, CX - 3, 1) for x in (v1, v2))
    below, a = new_at(0), new_at(1)
    b = second_field(below, a, v)
    carry = (a, (b[0][main], b[1][main]), advance_u(v))
    part = 8

    def store(k, c):
        there = pl.ds(pl.multiple_of((c * CZ + k * part) * CY, 8), part * CY)
        return pltpu.make_async_copy(out_v.at[there], out_hbm.at[there], store_sem.at[k, c])

    def chunk(k, carry):
        carry = lax.fori_loop(k * part, (k + 1) * part, level_two, carry)
        for c in range(3):
            store(k, c).start()
        return carry

    lax.fori_loop(0, CZ // part, chunk, carry)
    for k in range(CZ // part):
        for c in range(3):
            store(k, c).wait()


def f32(*shape):
    return jax.ShapeDtypeStruct(shape, jnp.float32)


def vmem(*shape):
    return pltpu.VMEM(shape, jnp.float32)


def local(side_field, magnetogram):
    side = side_field.reshape(2 * CZ * CY, CX)
    whole = pl.BlockSpec(memory_space=pltpu.VMEM)
    where_it_is = pl.BlockSpec(memory_space=pl.ANY)
    dma = pltpu.SemaphoreType.DMA
    ext, zh, q, e = pl.pallas_call(
        comm_kernel,
        out_shape=(f32(2 * EZ * 8, CX), f32(6 * CY, CX), f32(2 * EY, CX), f32(8 * EY, CX)),
        in_specs=[where_it_is, whole],
        out_specs=(whole,) * 4,
        scratch_shapes=[
            vmem(2 * LEVEL, CX),
            vmem(2 * CY, CX),
            vmem(UP, 2 * CY, CX),
            vmem(DOWN, 2 * CY, CX),
        ]
        + [vmem(4 * CZ, CX)] * 4
        + [vmem(16, CX)] * 4
        + [vmem(2 * EY, CX)] * 4
        + [
            vmem(8, CX),
            vmem(CY, CX),
            vmem(8 * (NY_DEV - 1), CX),
            vmem(CY * (NX_DEV - 1), CX),
            vmem(2 * CY, CX),
            vmem(16, CX),
            vmem(16, CX),
            vmem(16, CX),
            vmem(16, CX),
            vmem(2 * CY, CX),
            vmem(2 * CY, CX),
            vmem(4, 16, CX),
        ]
        + [dma((2,))]
        + [dma((UP, 2))] * 2
        + [dma((DOWN, 2))] * 2
        + [dma((2, 2))] * 2
        + [dma((2,))] * 6
        + [dma((NY_DEV - 1,))] * 2
        + [dma((NX_DEV - 1,))] * 2
        + [dma((8,))] * 2,
        compiler_params=pltpu.CompilerParams(collective_id=0, has_side_effects=True),
        name="exchange",
    )(side, magnetogram)
    out = pl.pallas_call(
        step_kernel,
        out_shape=f32(3 * CZ * CY, CX),
        in_specs=[where_it_is] + [whole] * 4,
        out_specs=where_it_is,
        scratch_shapes=[
            vmem(2 * LEVEL, CX),
            vmem(3 * (CZ + 2) * CY, CX),
            vmem(3 * (CZ + 2) * 8, CX),
            vmem(3 * CZ * CY, CX),
            dma((2,)),
            dma((CZ // 8, 3)),
        ],
        name="steps",
    )(side, ext, zh, q, e)
    return out.reshape(3, CZ, CY, CX)


def solution(mesh):
    return jax.shard_map(
        local,
        mesh=mesh,
        in_specs=(P(None, "gz", "gy", "gx"), P("gy", "gx")),
        out_specs=P(None, "gz", "gy", "gx"),
        check_vma=False,
    )
```

time: 122 us -> 50.2 us (0.41)
  Pallas kernels: 0 us -> 50 us
  other arithmetic: 46.6 us -> 0 us
  starting transfers between devices: 34.9 us -> 0 us
  waiting for transfers between devices: 22.3 us -> 0 us
  local copies, waits for them, and re-layouts: 16.9 us -> 0 us
    pallas_call x0 -> x2, Pallas kernels: none -> 50 us  [the longest x1 31 us: local(): pl.pallas_call(comm_kernel, out_shape=(f32(2 * EZ * 8, CX), f32(6 * CY, C...]
    another operation x7 -> x0, other arithmetic: 26.8 us -> none  [the longest x4 16.6 us: advance(): return inner + friction * jnp.stack([drive_x, drive_y, drive_z])]
    all_to_all x3 -> x0, starting transfers between devices: 18.4 us -> none  [from_everyone(): return lax.all_to_all(copies, axis, split_axis=0, concat_axis=0, tiled=True)]
    ppermute x6 -> x0, starting transfers between devices: 16.4 us -> none  [the longest x3 11.7 us: with_halo(): lax.ppermute(lax.slice_in_dim(block, block.shape[dim] - width, None, axis...]
    all_to_all x3 -> x0, waiting for transfers between devices: 14.5 us -> none  [from_everyone(): return lax.all_to_all(copies, axis, split_axis=0, concat_axis=0, tiled=True)]
    slice x11 -> x0, local copies, waits for them, and re-layouts: 7.76 us -> none  [the longest x2 5.06 us: with_halo(): lax.slice_in_dim(block, block.shape[dim] - width, None, axis=dim)]
    ppermute x6 -> x0, waiting for transfers between devices: 7.71 us -> none  [the longest x3 7.7 us: with_halo(): lax.ppermute(lax.slice_in_dim(block, 0, width, axis=dim), axis, backward)]
    concatenate x2 -> x0, other arithmetic: 6.41 us -> none  [with_halo(): block = jnp.concatenate([low, block, high], axis=dim)]
  transfers between devices with their start and end apart: 9 -> 0, of which waited for: 4 -> 0; matrix products, arithmetic and copies ran while one was open for 13% -> 0% of each run, Pallas kernels for 0% -> 0%
where the time goes in v1:
time: 50.2 us; the launch traced here: 50 us
  Pallas kernels  50 us (100%)
    pallas_call x1, Pallas kernels, local(): pl.pallas_call(comm_kernel, out_shape=(f32(2 * EZ * 8, CX), f32(6 * CY, C...  31 us
    pallas_call x1, Pallas kernels, local(): pl.pallas_call(step_kernel, out_shape=f32(3 * CZ * CY, CX), in_specs=[whe...  19 us

profile of v1, /device:TPU:1, one launch (start us, length us, event | category | flops | bytes accessed | tf_op | source)
XLA Modules:
  0.0 50.0 jit_solution(427528376826472776)
XLA Ops:
  0.0 31.0 %exchange.1 = (f32[816,128]{1,0:T(8,128)}, f32[192,128]{1,0:T(8,128)}, f32[80,128]{1,0:T(8,128)}, f32[320,128]{1,0:T(8,128)}) custom-call(f32[3072,128]{1,0:T(8,128)} %bitcast.2, f32[32,128]{1,0:T(8,128)} %mag_ref.1), custom_call_target="tpu_custom_call" | custom-call | tf_op jit(solution)/shard_map/exchange/pallas_call | solution.py:646
  31.0 19.0 %steps.1 = f32[4608,128]{1,0:T(8,128)} custom-call(f32[3072,128]{1,0:T(8,128)} %bitcast.3, f32[816,128]{1,0:T(8,128)} %get-tuple-element.9.ext_ref, f32[192,128]{1,0:T(8,128)} %get-tuple-element.10.zh_ref, f32[80,128]{1,0:T(8,128)} %get-tuple-element.11.q_ref, f32[320,128]{1,0:T(8,128)} %get-tuple-element.12.e_ref), custom_call_target="tpu_custom_call" | custom-call | tf_op jit(solution)/shard_map/steps/pallas_call | solution.py:685

commit v2 on v1

--- a/solution.py
+++ b/solution.py
@@ -16,7 +16,6 @@
 EZ = CZ + 3
 EY = CY + 8
 LEVEL = EZ * CY
-UP, DOWN = 4, 3
 
 
 def lanes(shape):
@@ -36,8 +35,7 @@
     e_out,
     side_v,
     t_v,
-    ring_up,
-    ring_dn,
+    tr,
     ys_lo,
     ys_hi,
     yr_lo,
@@ -50,6 +48,11 @@
     w_lo,
     wn_hi,
     wn_lo,
+    wt_lo,
+    wt_hi,
+    wy_lo,
+    wy_hi,
+    wd,
     mc_s,
     mr_s,
     mc_r,
@@ -63,10 +66,8 @@
     qx_hi,
     qd,
     load_sem,
-    s_up,
-    r_up,
-    s_dn,
-    r_dn,
+    s_t,
+    r_t,
     s_z,
     r_z,
     s_y,
@@ -94,6 +95,36 @@
             where["gx"] = lax.rem(gx + dx + NX_DEV, NX_DEV)
         return where
 
+    def there(dz=0, dy=0, dx=0):
+        ok = None
+        for here, d, size in ((gz, dz, NZ_DEV), (gy, dy, NY_DEV), (gx, dx, NX_DEV)):
+            if d:
+                one = here + d < size if d > 0 else here + d >= 0
+                ok = one if ok is None else jnp.logical_and(ok, one)
+        return ok
+
+    class Hop:
+        def __init__(self, src, dst, ssem, rsem, **by):
+            self.copy = pltpu.make_async_remote_copy(
+                src_ref=src,
+                dst_ref=dst,
+                send_sem=ssem,
+                recv_sem=rsem,
+                device_id=at(**by),
+                device_id_type=MESH,
+            )
+            self.to = there(**by)
+            self.back = there(**{k: -v for k, v in by.items()})
+
+        def start(self):
+            pl.when(self.to)(self.copy.start)
+
+        def wait_send(self):
+            pl.when(self.to)(self.copy.wait_send)
+
+        def wait_recv(self):
+            pl.when(self.back)(self.copy.wait_recv)
+
     loads = [
         pltpu.make_async_copy(
             side_hbm.at[pl.ds(c * CZ * CY, CZ * CY)],
@@ -106,30 +137,45 @@
         load.start()
 
     barrier = pltpu.get_barrier_semaphore()
-    peers = (
-        [at(dz=1), at(dz=-1)]
+    for peer in (
+        [at(dz=d) for d in range(1, NZ_DEV)]
         + [at(dy=d) for d in range(1, NY_DEV)]
         + [at(dx=d) for d in range(1, NX_DEV)]
-        + [at(dy=a, dx=b) for a in (1, -1) for b in (1, -1)]
-    )
-    for peer in peers:
+    ):
         pl.semaphore_signal(barrier, inc=1, device_id=peer, device_id_type=MESH)
-
-    def send(src, dst, ssem, rsem, where):
-        return pltpu.make_async_remote_copy(
-            src_ref=src,
-            dst_ref=dst,
-            send_sem=ssem,
-            recv_sem=rsem,
-            device_id=where,
-            device_id_type=MESH,
-        )
+    diagonal = [dict(dy=a, dx=b) for a in (1, -1) for b in (1, -1)]
+    greeted = jnp.int32(NZ_DEV + NY_DEV + NX_DEV - 3)
+    for by in diagonal:
+        greeted = greeted + there(**by).astype(jnp.int32)
+
+        @pl.when(there(**by))
+        def _(by=by):
+            pl.semaphore_signal(barrier, inc=1, device_id=at(**by), device_id_type=MESH)
 
     mag = mag_ref[...]
     mc_s[...] = jnp.broadcast_to(jnp.sum(mag, axis=0, keepdims=True), (8, CX))
     mr_s[...] = jnp.broadcast_to(jnp.sum(mag, axis=1, keepdims=True), (CY, CX))
     ext_out[...] = jnp.zeros_like(ext_out)
 
+    def clear(by, *refs):
+        @pl.when(jnp.logical_not(there(**by)))
+        def _():
+            for ref in refs:
+                ref[...] = jnp.zeros_like(ref)
+
+    clear(dict(dz=-1), side_v.at[pl.ds(0, CY)], side_v.at[pl.ds(LEVEL, CY)])
+    clear(
+        dict(dz=1),
+        side_v.at[pl.ds((CZ + 1) * CY, 2 * CY)],
+        side_v.at[pl.ds(LEVEL + (CZ + 1) * CY, 2 * CY)],
+    )
+    clear(dict(dy=-1), yr_lo, cr_lo, wy_lo, qy_lo)
+    clear(dict(dy=1), yr_hi, cr_hi, wy_hi, qy_hi)
+    clear(dict(dx=-1), wn_lo, qx_lo)
+    clear(dict(dx=1), wn_hi, qx_hi)
+    for i, by in enumerate((dict(dy=1, dx=-1), dict(dy=1, dx=1), dict(dy=-1, dx=-1), dict(dy=-1, dx=1))):
+        clear(by, wd.at[i], qd.at[i])
+
     for c in range(2):
         loads[c].wait()
 
@@ -139,57 +185,45 @@
         t_v[pl.ds(c * CY, CY), :] = lax.fori_loop(
             0, CZ, add, jnp.zeros((CY, CX), jnp.float32), unroll=8
         )
-    pl.semaphore_wait(barrier, len(peers))
-
-    def up(s, c):
-        src = t_v.at[pl.ds(c * CY, CY)] if s == 0 else ring_up.at[s - 1, pl.ds(c * CY, CY)]
-        return send(
-            src, ring_up.at[s, pl.ds(c * CY, CY)], s_up.at[s, c], r_up.at[s, c], at(dz=1)
-        )
-
-    def down(s, c):
-        src = t_v.at[pl.ds(c * CY, CY)] if s == 0 else ring_dn.at[s - 1, pl.ds(c * CY, CY)]
-        return send(
-            src, ring_dn.at[s, pl.ds(c * CY, CY)], s_dn.at[s, c], r_dn.at[s, c], at(dz=-1)
-        )
-
-    ups = [[up(s, c) for c in range(2)] for s in range(UP)]
-    downs = [[down(s, c) for c in range(2)] for s in range(DOWN)]
-    for c in range(2):
-        ups[0][c].start()
-        downs[0][c].start()
-
-    sums = [
-        send(mc_s, mc_r.at[pl.ds(8 * (d - 1), 8)], s_mc.at[d - 1], r_mc.at[d - 1], at(dy=d))
-        for d in range(1, NY_DEV)
-    ] + [
-        send(mr_s, mr_r.at[pl.ds(CY * (d - 1), CY)], s_mr.at[d - 1], r_mr.at[d - 1], at(dx=d))
-        for d in range(1, NX_DEV)
-    ]
-    for one in sums:
-        one.start()
+    pl.semaphore_wait(barrier, greeted)
 
     layers = []
     for c in range(2):
         layers.append(
-            send(
+            Hop(
                 side_hbm.at[pl.ds(c * CZ * CY + (CZ - 1) * CY, CY)],
                 side_v.at[pl.ds(c * LEVEL, CY)],
                 s_z.at[0, c],
                 r_z.at[0, c],
-                at(dz=1),
+                dz=1,
             )
         )
         layers.append(
-            send(
+            Hop(
                 side_hbm.at[pl.ds(c * CZ * CY, 2 * CY)],
                 side_v.at[pl.ds(c * LEVEL + (CZ + 1) * CY, 2 * CY)],
                 s_z.at[1, c],
                 r_z.at[1, c],
-                at(dz=-1),
+                dz=-1,
             )
         )
     for one in layers:
+        one.start()
+
+    ups = [
+        Hop(t_v, tr.at[d - 1], s_t.at[d - 1], r_t.at[d - 1], dz=d) for d in (4, 5, 3, 6, 2, 7, 1)
+    ]
+    for one in ups:
+        one.start()
+
+    sums = [
+        Hop(mc_s, mc_r.at[pl.ds(8 * (d - 1), 8)], s_mc.at[d - 1], r_mc.at[d - 1], dy=d)
+        for d in range(1, NY_DEV)
+    ] + [
+        Hop(mr_s, mr_r.at[pl.ds(CY * (d - 1), CY)], s_mr.at[d - 1], r_mr.at[d - 1], dx=d)
+        for d in range(1, NX_DEV)
+    ]
+    for one in sums:
         one.start()
 
     for c in range(2):
@@ -198,26 +232,61 @@
             ys_lo[here, :] = side_v[pl.ds(c * LEVEL + CY + k, CZ, stride=CY), :]
             ys_hi[here, :] = side_v[pl.ds(c * LEVEL + CY + CY - 2 + k, CZ, stride=CY), :]
     faces = [
-        send(ys_lo, yr_hi, s_y.at[0], r_y.at[0], at(dy=-1)),
-        send(ys_hi, yr_lo, s_y.at[1], r_y.at[1], at(dy=1)),
+        Hop(ys_lo, yr_hi, s_y.at[0], r_y.at[0], dy=-1),
+        Hop(ys_hi, yr_lo, s_y.at[1], r_y.at[1], dy=1),
     ]
     for one in faces:
         one.start()
 
-    def pass_on(s):
+    main_lane = lanes((CY, CX))
+
+    def main(c, level):
+        return side_v[pl.ds(pl.multiple_of(c * LEVEL + level * CY, 8), CY), :]
+
+    def place(zi, running, packed):
+        first = 2 * zi
+        out = []
         for c in range(2):
-            ups[s][c].wait_recv()
-            if s + 1 < UP:
-                ups[s + 1][c].start()
-            if s < DOWN:
-                downs[s][c].wait_recv()
-                if s + 1 < DOWN:
-                    downs[s + 1][c].start()
-
-    pass_on(0)
+            turned = pltpu.roll(running[c], first + 2, 1)
+            hi, lo = packed[2 * c], packed[2 * c + 1]
+            out.append(jnp.where((main_lane == first) | (main_lane == first + 1), turned, hi))
+            out.append(jnp.where((main_lane == first + 2) | (main_lane == first + 3), turned, lo))
+        return tuple(out)
+
+    nothing = jnp.zeros((CY, CX), jnp.float32)
+
+    def pack(zi, carry):
+        running, packed = carry
+        running = tuple(running[c] + main(c, zi - 1) for c in range(2))
+        return running, place(zi, running, packed)
+
+    running, packed = lax.fori_loop(
+        2, CZ + 2, pack, ((nothing,) * 2, (nothing,) * 4), unroll=4
+    )
 
     for one in layers:
         one.wait_recv()
+    for zi in (CZ + 2, CZ + 3):
+        running, packed = pack(zi, (running, packed))
+    packed = place(0, tuple(-main(c, 0) for c in range(2)), packed)
+    for c in range(2):
+        for k, (ref, x) in enumerate(((w_hi, packed[2 * c]), (w_lo, packed[2 * c + 1]))):
+            ref[pl.ds(c * CY, CY), :] = x
+            wt_lo[pl.ds((2 * k + c) * 8, 8), :] = x[:8]
+            wt_hi[pl.ds((2 * k + c) * 8, 8), :] = x[CY - 8 :]
+    columns = [
+        Hop(w_hi, wn_lo, s_w.at[0], r_w.at[0], dx=1),
+        Hop(w_lo, wn_hi, s_w.at[1], r_w.at[1], dx=-1),
+        Hop(wt_lo, wy_hi, s_w.at[2], r_w.at[2], dy=-1),
+        Hop(wt_hi, wy_lo, s_w.at[3], r_w.at[3], dy=1),
+        Hop(wt_lo.at[pl.ds(0, 16)], wd.at[0], s_w.at[4], r_w.at[4], dy=-1, dx=1),
+        Hop(wt_lo.at[pl.ds(16, 16)], wd.at[1], s_w.at[5], r_w.at[5], dy=-1, dx=-1),
+        Hop(wt_hi.at[pl.ds(0, 16)], wd.at[2], s_w.at[6], r_w.at[6], dy=1, dx=1),
+        Hop(wt_hi.at[pl.ds(16, 16)], wd.at[3], s_w.at[7], r_w.at[7], dy=1, dx=-1),
+    ]
+    for one in columns:
+        one.start()
+
     for c in range(2):
         for i, level in enumerate((0, CZ + 1, CZ + 2)):
             first = c * LEVEL + level * CY
@@ -228,79 +297,12 @@
     cs_lo[pl.ds(12, 4), :] = jnp.zeros((4, CX), jnp.float32)
     cs_hi[pl.ds(12, 4), :] = jnp.zeros((4, CX), jnp.float32)
     corners = [
-        send(cs_lo, cr_hi, s_c.at[0], r_c.at[0], at(dy=-1)),
-        send(cs_hi, cr_lo, s_c.at[1], r_c.at[1], at(dy=1)),
+        Hop(cs_lo, cr_hi, s_c.at[0], r_c.at[0], dy=-1),
+        Hop(cs_hi, cr_lo, s_c.at[1], r_c.at[1], dy=1),
     ]
     for one in corners:
         one.start()
 
-    has_ylo = (gy > 0).astype(jnp.float32)
-    has_yhi = (gy < NY_DEV - 1).astype(jnp.float32)
-    has_xlo = (gx > 0).astype(jnp.float32)
-    has_xhi = (gx < NX_DEV - 1).astype(jnp.float32)
-
-    for one in faces:
-        one.wait_recv()
-    for c in range(2):
-        for k in range(2):
-            here = pl.ds((2 * c + k) * CZ, CZ)
-            ext_out[pl.ds((c * EZ + 1) * 8 + k, CZ, stride=8), :] = yr_hi[here, :] * has_yhi
-            ext_out[pl.ds((c * EZ + 1) * 8 + 6 + k, CZ, stride=8), :] = yr_lo[here, :] * has_ylo
-
-    pass_on(1)
-
-    for one in corners:
-        one.wait_recv()
-    for c in range(2):
-        for i, level in enumerate((0, CZ + 1, CZ + 2)):
-            first = (c * EZ + level) * 8
-            of = (c * 3 + i) * 2
-            ext_out[pl.ds(first, 2), :] = cr_hi[pl.ds(of, 2), :] * has_yhi
-            ext_out[pl.ds(first + 6, 2), :] = cr_lo[pl.ds(of, 2), :] * has_ylo
-
-    lane = lanes((EY, CX))
-
-    def raw(c, level):
-        return jnp.concatenate(
-            [
-                side_v[pl.ds(pl.multiple_of(c * LEVEL + level * CY, 8), CY), :],
-                ext_out[pl.ds(pl.multiple_of((c * EZ + level) * 8, 8), 8), :],
-            ],
-            axis=0,
-        )
-
-    def place(zi, running, packed):
-        first = 2 * zi
-        out = []
-        for c in range(2):
-            turned = pltpu.roll(running[c], first + 2, 1)
-            hi, lo = packed[2 * c], packed[2 * c + 1]
-            out.append(jnp.where((lane == first) | (lane == first + 1), turned, hi))
-            out.append(jnp.where((lane == first + 2) | (lane == first + 3), turned, lo))
-        return tuple(out)
-
-    nothing = jnp.zeros((EY, CX), jnp.float32)
-    running = tuple(-raw(c, 0) for c in range(2))
-    packed = place(0, running, (nothing,) * 4)
-
-    def pack(zi, carry):
-        running, packed = carry
-        running = tuple(running[c] + raw(c, zi - 1) for c in range(2))
-        return running, place(zi, running, packed)
-
-    _, packed = lax.fori_loop(1, EZ + 1, pack, (running, packed))
-    for c in range(2):
-        w_hi[pl.ds(c * EY, EY), :] = packed[2 * c]
-        w_lo[pl.ds(c * EY, EY), :] = packed[2 * c + 1]
-    columns = [
-        send(w_hi, wn_lo, s_w.at[0], r_w.at[0], at(dx=1)),
-        send(w_lo, wn_hi, s_w.at[1], r_w.at[1], at(dx=-1)),
-    ]
-    for one in columns:
-        one.start()
-
-    for one in sums:
-        one.wait_recv()
     col = mag
     row_of = rows((CY, CX))
     for k in (1, 2, 4, 8, 16):
@@ -309,91 +311,124 @@
     lane_of = lanes((CY, CX))
     for k in (1, 2, 4, 8, 16, 32, 64):
         lin = lin + jnp.where(lane_of >= k, pltpu.roll(lin, k, 1), 0.0)
-    for d in range(1, NY_DEV):
-        part = mc_r[pl.ds(8 * (d - 1), 1), :]
-        col = col + jnp.where(d <= gy, part, 0.0)
-    for d in range(1, NX_DEV):
-        part = mr_r[pl.ds(CY * (d - 1), CY), :]
-        lin = lin + jnp.where(d <= gx, part, 0.0)
-    base = (-0.5 * spacing * col, 0.5 * spacing * lin)
-
-    pass_on(2)
-    below = [jnp.zeros((CY, CX), jnp.float32) for _ in range(2)]
-    for c in range(2):
-        for s in range(3):
-            part = ring_up[s, pl.ds(c * CY, CY), :]
-            below[c] = below[c] + jnp.where(gz - (s + 1) >= 0, part, 0.0)
-            part = ring_dn[s, pl.ds(c * CY, CY), :]
-            below[c] = below[c] + jnp.where(gz + (s + 1) >= NZ_DEV, part, 0.0)
-
-    for one in columns:
+    q_v[pl.ds(0, CY), :] = col
+    q_v[pl.ds(CY, CY), :] = lin
+    for d, one in enumerate(sums[: NY_DEV - 1]):
+
+        @pl.when(one.back)
+        def _(d=d, one=one):
+            one.wait_recv()
+            q_v[pl.ds(0, CY), :] = q_v[pl.ds(0, CY), :] + mc_r[pl.ds(8 * d, 1), :]
+
+    for d, one in enumerate(sums[NY_DEV - 1 :]):
+
+        @pl.when(one.back)
+        def _(d=d, one=one):
+            one.wait_recv()
+            q_v[pl.ds(CY, CY), :] = q_v[pl.ds(CY, CY), :] + mr_r[pl.ds(CY * d, CY), :]
+
+    q_v[pl.ds(0, CY), :] = (-0.5 * spacing) * q_v[pl.ds(0, CY), :]
+    q_v[pl.ds(CY, CY), :] = (0.5 * spacing) * q_v[pl.ds(CY, CY), :]
+
+    for one in faces:
         one.wait_recv()
-
-    pass_on(3)
-    for c in range(2):
-        part = ring_up[3, pl.ds(c * CY, CY), :]
-        below[c] = below[c] + jnp.where(gz - 4 >= 0, part, 0.0)
-    q = (base[0] + spacing * below[1], base[1] - spacing * below[0])
-    for c in range(2):
-        q_v[pl.ds(c * CY, CY), :] = q[c]
+    for c in range(2):
+        for k in range(2):
+            here = pl.ds((2 * c + k) * CZ, CZ)
+            ext_out[pl.ds((c * EZ + 1) * 8 + k, CZ, stride=8), :] = yr_hi[here, :]
+            ext_out[pl.ds((c * EZ + 1) * 8 + 6 + k, CZ, stride=8), :] = yr_lo[here, :]
+
+    for one in ups:
+
+        @pl.when(one.back)
+        def _(one=one):
+            one.wait_recv()
+
+    for d in range(1, NZ_DEV):
+
+        @pl.when(there(dz=-d))
+        def _(d=d):
+            q_v[pl.ds(0, CY), :] = q_v[pl.ds(0, CY), :] + spacing * tr[d - 1, pl.ds(CY, CY), :]
+            q_v[pl.ds(CY, CY), :] = q_v[pl.ds(CY, CY), :] - spacing * tr[d - 1, pl.ds(0, CY), :]
+
+    q = tuple(q_v[pl.ds(c * CY, CY), :] for c in range(2))
+    for c in range(2):
         qt_lo[pl.ds(c * 8, 8), :] = q[c][:8]
         qt_hi[pl.ds(c * 8, 8), :] = q[c][CY - 8 :]
     planes = [
-        send(q_v, qx_lo, s_q.at[0], r_q.at[0], at(dx=1)),
-        send(q_v, qx_hi, s_q.at[1], r_q.at[1], at(dx=-1)),
-        send(qt_lo, qy_hi, s_q.at[2], r_q.at[2], at(dy=-1)),
-        send(qt_hi, qy_lo, s_q.at[3], r_q.at[3], at(dy=1)),
-        send(qt_lo, qd.at[0], s_q.at[4], r_q.at[4], at(dy=-1, dx=1)),
-        send(qt_lo, qd.at[1], s_q.at[5], r_q.at[5], at(dy=-1, dx=-1)),
-        send(qt_hi, qd.at[2], s_q.at[6], r_q.at[6], at(dy=1, dx=1)),
-        send(qt_hi, qd.at[3], s_q.at[7], r_q.at[7], at(dy=1, dx=-1)),
+        Hop(q_v, qx_lo, s_q.at[0], r_q.at[0], dx=1),
+        Hop(q_v, qx_hi, s_q.at[1], r_q.at[1], dx=-1),
+        Hop(qt_lo, qy_hi, s_q.at[2], r_q.at[2], dy=-1),
+        Hop(qt_hi, qy_lo, s_q.at[3], r_q.at[3], dy=1),
+        Hop(qt_lo, qd.at[0], s_q.at[4], r_q.at[4], dy=-1, dx=1),
+        Hop(qt_lo, qd.at[1], s_q.at[5], r_q.at[5], dy=-1, dx=-1),
+        Hop(qt_hi, qd.at[2], s_q.at[6], r_q.at[6], dy=1, dx=1),
+        Hop(qt_hi, qd.at[3], s_q.at[7], r_q.at[7], dy=1, dx=-1),
     ]
     for one in planes:
         one.start()
+
+    for one in corners:
+        one.wait_recv()
+    for c in range(2):
+        for i, level in enumerate((0, CZ + 1, CZ + 2)):
+            first = (c * EZ + level) * 8
+            of = (c * 3 + i) * 2
+            ext_out[pl.ds(first, 2), :] = cr_hi[pl.ds(of, 2), :]
+            ext_out[pl.ds(first + 6, 2), :] = cr_lo[pl.ds(of, 2), :]
+
+    row8 = rows((8, CX))
+
+    def plane(middle, from_hi, from_lo):
+        tile = jnp.where(row8 < 2, from_hi, jnp.where(row8 >= 6, from_lo, 0.0))
+        return jnp.concatenate([middle, tile], axis=0)
+
+    for one in columns:
+        one.wait_recv()
+
+    lane = lanes((EY, CX))
+    even = lane % 2 == 0
+    level_ok = ((lane >= 4) | (gz > 0)) & ((lane < 2 * (CZ + 2)) | (gz < NZ_DEV - 1))
+    grown = []
+    for c in range(2):
+        o, sign = (1, spacing) if c == 0 else (0, -spacing)
+        mine, tile = pl.ds(o * CY, CY), pl.ds(o * 8, 8)
+        other = pl.ds(16 + o * 8, 8)
+        hi = plane(w_hi[mine, :], wy_hi[tile, :], wy_lo[tile, :])
+        lo = plane(w_lo[mine, :], wy_hi[other, :], wy_lo[other, :])
+        lon = plane(wn_lo[mine, :], wd[0, tile, :], wd[2, tile, :])
+        hin = plane(wn_hi[mine, :], wd[1, tile, :], wd[3, tile, :])
+        pairs = (
+            (hi, pltpu.roll(lon, 1, 1)),
+            (pltpu.roll(hi, CX - 1, 1), lon),
+            (pltpu.roll(hin, CX - 2, 1), pltpu.roll(lo, CX - 1, 1)),
+            (pltpu.roll(hin, CX - 3, 1), pltpu.roll(lo, CX - 2, 1)),
+        )
+        grown.append([sign * jnp.where(even, *pair) for pair in pairs])
+
     for one in planes:
         one.wait_recv()
-
-    row8 = rows((8, CX))
-
-    def fifth(from_hi, from_lo):
-        return jnp.where(
-            row8 < 2, from_hi * has_yhi, jnp.where(row8 >= 6, from_lo * has_ylo, 0.0)
-        )
-
-    def plane(main, from_hi, from_lo, c):
-        tile = fifth(from_hi[pl.ds(c * 8, 8), :], from_lo[pl.ds(c * 8, 8), :])
-        return jnp.concatenate([main, tile], axis=0)
-
-    even = lane % 2 == 0
-    level_ok = ((lane >= 4) | (gz > 0)) & ((lane < 2 * (CZ + 2)) | (gz < NZ_DEV - 1))
-    for c in range(2):
-        own = plane(q[c], qy_hi, qy_lo, c)
-        low = plane(qx_lo[pl.ds(c * CY, CY), :], qd.at[0], qd.at[2], c) * has_xlo
-        high = plane(qx_hi[pl.ds(c * CY, CY), :], qd.at[1], qd.at[3], c) * has_xhi
+    for c in range(2):
+        tile = pl.ds(c * 8, 8)
+        own = plane(q[c], qy_hi[tile, :], qy_lo[tile, :])
+        low = plane(qx_lo[pl.ds(c * CY, CY), :], qd[0, tile, :], qd[2, tile, :])
+        high = plane(qx_hi[pl.ds(c * CY, CY), :], qd[1, tile, :], qd[3, tile, :])
         q_out[pl.ds(c * EY, EY), :] = own
-
-        o, sign = (1, spacing) if c == 0 else (0, -spacing)
-        there = pl.ds(o * EY, EY)
-        hi, lo = w_hi[there, :], w_lo[there, :]
-        hin, lon = wn_hi[there, :] * has_xhi, wn_lo[there, :] * has_xlo
 
         def spread(x, i):
             return jnp.broadcast_to(x[:, i : i + 1], (EY, CX))
 
-        parts = (
-            (spread(own, 126), spread(low, 126), hi, pltpu.roll(lon, 1, 1)),
-            (spread(own, 127), spread(low, 127), pltpu.roll(hi, CX - 1, 1), lon),
-            (spread(high, 0), spread(own, 0), pltpu.roll(hin, CX - 2, 1), pltpu.roll(lo, CX - 1, 1)),
-            (spread(high, 1), spread(own, 1), pltpu.roll(hin, CX - 3, 1), pltpu.roll(lo, CX - 2, 1)),
-        )
-        for m, (q_hi, q_lo, l_hi, l_lo) in enumerate(parts):
-            value = jnp.where(even, q_hi, q_lo) + sign * jnp.where(even, l_hi, l_lo)
+        sides = (
+            (spread(own, 126), spread(low, 126)),
+            (spread(own, 127), spread(low, 127)),
+            (spread(high, 0), spread(own, 0)),
+            (spread(high, 1), spread(own, 1)),
+        )
+        for m, pair in enumerate(sides):
+            value = jnp.where(even, *pair) + grown[c][m]
             e_out[pl.ds((m * 2 + c) * EY, EY), :] = jnp.where(level_ok, value, 0.0)
 
-    for group in ups + downs:
-        for one in group:
-            one.wait_send()
-    for one in sums + layers + faces + corners + columns + planes:
+    for one in ups + sums + layers + faces + corners + columns + planes:
         one.wait_send()
 
 
@@ -553,13 +588,15 @@
     u = advance_u(u)
 
     def level_one(z, carry):
-        a, before, u = carry
+        a, before = carry
         a_up = grow(a, z + 2)
+        u = tuple(pltpu.roll(x, lax.rem(2 * CX - 1 - 2 * (z + 2), CX), 1) for x in (u1, u2))
         b = field_at(a, a_up, u)
         first_step(a, b, before, u, z + 1)
-        return a_up, (b[0], b[1]), advance_u(u)
-
-    a, before, u = lax.fori_loop(0, CZ - 1, level_one, (a, (b[0], b[1]), u))
+        return a_up, (b[0], b[1])
+
+    a, before = lax.fori_loop(0, CZ - 1, level_one, (a, (b[0], b[1])), unroll=4)
+    u = tuple(turn(x, CX - 1 - 2 * (CZ + 1), 1) for x in (u1, u2))
     top = tuple(x * in_hi for x in grow(a, CZ + 1))
     b = field_at(a, top, u)
     first_step(a, b, before, u, CZ)
@@ -593,7 +630,8 @@
     first_main, main = first_lane[:CY], slice(0, CY)
 
     def level_two(z, carry):
-        a, before, v = carry
+        a, before = carry
+        v = tuple(pltpu.roll(x, lax.rem(2 * CX - 1 - 2 * (z + 2), CX), 1) for x in (v1, v2))
         a_up = new_at(z + 2)
         b = second_field(a, a_up, v)
         ym = (turn(b[0], 1, 0)[main], None, turn(b[2], 1, 0)[main])
@@ -606,12 +644,12 @@
         d = drive(own, before, ym, xm)
         for c in range(3):
             out_v[pl.ds(pl.multiple_of((c * CZ + z) * CY, 8), CY), :] = a[c][main] + d[c]
-        return a_up, (own[0], own[1]), advance_u(v)
+        return a_up, (own[0], own[1])
 
     v = tuple(turn(x, CX - 3, 1) for x in (v1, v2))
     below, a = new_at(0), new_at(1)
     b = second_field(below, a, v)
-    carry = (a, (b[0][main], b[1][main]), advance_u(v))
+    carry = (a, (b[0][main], b[1][main]))
     part = 8
 
     def store(k, c):
@@ -619,7 +657,7 @@
         return pltpu.make_async_copy(out_v.at[there], out_hbm.at[there], store_sem.at[k, c])
 
     def chunk(k, carry):
-        carry = lax.fori_loop(k * part, (k + 1) * part, level_two, carry)
+        carry = lax.fori_loop(0, part, lambda i, x: level_two(k * part + i, x), carry, unroll=4)
         for c in range(3):
             store(k, c).start()
         return carry
@@ -651,13 +689,14 @@
         scratch_shapes=[
             vmem(2 * LEVEL, CX),
             vmem(2 * CY, CX),
-            vmem(UP, 2 * CY, CX),
-            vmem(DOWN, 2 * CY, CX),
+            vmem(NZ_DEV - 1, 2 * CY, CX),
         ]
         + [vmem(4 * CZ, CX)] * 4
         + [vmem(16, CX)] * 4
-        + [vmem(2 * EY, CX)] * 4
+        + [vmem(2 * CY, CX)] * 4
+        + [vmem(32, CX)] * 4
         + [
+            vmem(4, 16, CX),
             vmem(8, CX),
             vmem(CY, CX),
             vmem(8 * (NY_DEV - 1), CX),
@@ -672,10 +711,10 @@
             vmem(4, 16, CX),
         ]
         + [dma((2,))]
-        + [dma((UP, 2))] * 2
-        + [dma((DOWN, 2))] * 2
+        + [dma((NZ_DEV - 1,))] * 2
         + [dma((2, 2))] * 2
-        + [dma((2,))] * 6
+        + [dma((2,))] * 4
+        + [dma((8,))] * 2
         + [dma((NY_DEV - 1,))] * 2
         + [dma((NX_DEV - 1,))] * 2
         + [dma((8,))] * 2,

time: 50.2 us -> 31.7 us (0.63)
  Pallas kernels: 50 us -> 31.5 us
    pallas_call x1, Pallas kernels: 31 us -> 21.4 us  [local(): pl.pallas_call(comm_kernel, out_shape=(f32(2 * EZ * 8, CX), f32(6 * CY, C...]
    pallas_call x1, Pallas kernels: 19 us -> 10.1 us  [local(): pl.pallas_call(step_kernel, out_shape=f32(3 * CZ * CY, CX), in_specs=[whe...]
where the time goes in v2:
time: 31.7 us; the launch traced here: 31.5 us
  Pallas kernels  31.5 us (99%)
    pallas_call x1, Pallas kernels, local(): pl.pallas_call(comm_kernel, out_shape=(f32(2 * EZ * 8, CX), f32(6 * CY, C...  21.4 us
    pallas_call x1, Pallas kernels, local(): pl.pallas_call(step_kernel, out_shape=f32(3 * CZ * CY, CX), in_specs=[whe...  10.1 us

profile of v2, /device:TPU:1, one launch (start us, length us, event | category | flops | bytes accessed | tf_op | source)
XLA Modules:
  0.0 31.5 jit_solution(5824976603949808308)
XLA Ops:
  0.0 21.4 %exchange.1 = (f32[816,128]{1,0:T(8,128)}, f32[192,128]{1,0:T(8,128)}, f32[80,128]{1,0:T(8,128)}, f32[320,128]{1,0:T(8,128)}) custom-call(f32[3072,128]{1,0:T(8,128)} %bitcast.2, f32[32,128]{1,0:T(8,128)} %mag_ref.1), custom_call_target="tpu_custom_call" | custom-call | tf_op jit(solution)/shard_map/exchange/pallas_call | solution.py:684
  21.4 10.1 %steps.1 = f32[4608,128]{1,0:T(8,128)} custom-call(f32[3072,128]{1,0:T(8,128)} %bitcast.3, f32[816,128]{1,0:T(8,128)} %get-tuple-element.9.ext_ref, f32[192,128]{1,0:T(8,128)} %get-tuple-element.10.zh_ref, f32[80,128]{1,0:T(8,128)} %get-tuple-element.11.q_ref, f32[320,128]{1,0:T(8,128)} %get-tuple-element.12.e_ref), custom_call_target="tpu_custom_call" | custom-call | tf_op jit(solution)/shard_map/steps/pallas_call | solution.py:724

commit v3 on v2

v3 whole, which is shorter than its diff:
```python
import functools

import jax
import jax.numpy as jnp
from jax import lax
from jax.experimental import pallas as pl
from jax.experimental.pallas import tpu as pltpu
from jax.sharding import PartitionSpec as P

spacing = 0.0625
friction = 0.004
MESH = pl.DeviceIdType.MESH

VMEM_BYTES = 24 * 2**20
UNROLL_PRE, UNROLL_STRIP, UNROLL_POST, UNROLL_EDGE, UNROLL_PACK = 8, 8, 4, 25, 8
NZ_DEV, NY_DEV, NX_DEV = 8, 8, 4
CZ, CY, CX = 48, 32, 128
EZ = CZ + 3
EY = CY + 8
LEVEL = EZ * CY


def lanes(shape):
    return lax.broadcasted_iota(jnp.int32, shape, len(shape) - 1)


def rows(shape):
    return lax.broadcasted_iota(jnp.int32, shape, len(shape) - 2)


def turn(x, shift, axis):
    return pltpu.roll(x, shift % x.shape[axis], axis)


def fields(a, zp, yp, xp, first):
    ax, ay = a[0], a[1]
    if first:
        bx = ay - zp[1]
        by = zp[0] - ax
    else:
        bx = (yp[2] - a[2]) - (zp[1] - ay)
        by = (zp[0] - ax) - (xp[2] - a[2])
    bz = (xp[1] - ay) - (yp[0] - ax)
    return bx, by, bz


def drive(b, zm, ym, xm):
    bx, by, bz = b
    jx = (bz - ym[2]) - (by - zm[1])
    jy = (bx - zm[0]) - (bz - xm[2])
    jz = (by - xm[1]) - (bx - ym[0])
    return push(b, (jx, jy, jz))


def push(b, j):
    bx, by, bz = b
    jx, jy, jz = j
    square = bx * bx + by * by + bz * bz
    scale = (friction / spacing**2) / (square + spacing**2)
    along = (jx * bx + jy * by + jz * bz) * scale
    across = square * scale
    return (along * bx - across * jx, along * by - across * jy, along * bz - across * jz)


def comm_kernel(
    side_hbm,
    mag_ref,
    a1_out,
    v_out,
    ext_v,
    pre_m,
    pre_e,
    side_v,
    t_v,
    tr,
    ys_lo,
    ys_hi,
    yr_lo,
    yr_hi,
    cs_lo,
    cs_hi,
    cr_lo,
    cr_hi,
    w_hi,
    w_lo,
    wn_hi,
    wn_lo,
    wt_lo,
    wt_hi,
    wy_lo,
    wy_hi,
    wd,
    mc_s,
    mr_s,
    mc_r,
    mr_r,
    q_v,
    qt_lo,
    qt_hi,
    qy_lo,
    qy_hi,
    load_sem,
    s_t,
    r_t,
    s_z,
    r_z,
    s_y,
    r_y,
    s_c,
    r_c,
    s_w,
    r_w,
    s_mc,
    r_mc,
    s_mr,
    r_mr,
    s_q,
    r_q,
):
    gz, gy, gx = lax.axis_index("gz"), lax.axis_index("gy"), lax.axis_index("gx")

    def at(dz=0, dy=0, dx=0):
        where = {}
        if dz:
            where["gz"] = lax.rem(gz + dz + NZ_DEV, NZ_DEV)
        if dy:
            where["gy"] = lax.rem(gy + dy + NY_DEV, NY_DEV)
        if dx:
            where["gx"] = lax.rem(gx + dx + NX_DEV, NX_DEV)
        return where

    def there(dz=0, dy=0, dx=0):
        ok = None
        for here, d, size in ((gz, dz, NZ_DEV), (gy, dy, NY_DEV), (gx, dx, NX_DEV)):
            if d:
                one = here + d < size if d > 0 else here + d >= 0
                ok = one if ok is None else jnp.logical_and(ok, one)
        return ok

    class Hop:
        def __init__(self, src, dst, ssem, rsem, **by):
            self.copy = pltpu.make_async_remote_copy(
                src_ref=src,
                dst_ref=dst,
                send_sem=ssem,
                recv_sem=rsem,
                device_id=at(**by),
                device_id_type=MESH,
            )
            self.to = there(**by)
            self.back = there(**{k: -v for k, v in by.items()})

        def start(self):
            pl.when(self.to)(self.copy.start)

        def wait_send(self):
            pl.when(self.to)(self.copy.wait_send)

        def wait_recv(self):
            pl.when(self.back)(self.copy.wait_recv)

    loads = [
        pltpu.make_async_copy(
            side_hbm.at[pl.ds(c * CZ * CY, CZ * CY)],
            side_v.at[pl.ds(c * LEVEL + CY, CZ * CY)],
            load_sem.at[c],
        )
        for c in range(2)
    ]
    for load in loads:
        load.start()

    barrier = pltpu.get_barrier_semaphore()
    for peer in (
        [at(dz=d) for d in range(1, NZ_DEV)]
        + [at(dy=d) for d in range(1, NY_DEV)]
        + [at(dx=d) for d in range(1, NX_DEV)]
    ):
        pl.semaphore_signal(barrier, inc=1, device_id=peer, device_id_type=MESH)
    diagonal = [dict(dy=a, dx=b) for a in (1, -1) for b in (1, -1)]
    greeted = jnp.int32(NZ_DEV + NY_DEV + NX_DEV - 3)
    for by in diagonal:
        greeted = greeted + there(**by).astype(jnp.int32)

        @pl.when(there(**by))
        def _(by=by):
            pl.semaphore_signal(barrier, inc=1, device_id=at(**by), device_id_type=MESH)

    mag = mag_ref[...]
    mc_s[...] = jnp.broadcast_to(jnp.sum(mag, axis=0, keepdims=True), (8, CX))
    mr_s[...] = jnp.broadcast_to(jnp.sum(mag, axis=1, keepdims=True), (CY, CX))

    def clear(by, *refs):
        @pl.when(jnp.logical_not(there(**by)))
        def _():
            for ref in refs:
                ref[...] = jnp.zeros_like(ref)

    clear(dict(dz=-1), side_v.at[pl.ds(0, CY)], side_v.at[pl.ds(LEVEL, CY)])
    clear(
        dict(dz=1),
        side_v.at[pl.ds((CZ + 1) * CY, 2 * CY)],
        side_v.at[pl.ds(LEVEL + (CZ + 1) * CY, 2 * CY)],
    )
    clear(dict(dy=-1), yr_lo, cr_lo, wy_lo, qy_lo)
    clear(dict(dy=1), yr_hi, cr_hi, wy_hi, qy_hi)
    clear(dict(dx=-1), wn_lo)
    clear(dict(dx=1), wn_hi)
    for i, by in enumerate((dict(dy=1, dx=-1), dict(dy=1, dx=1), dict(dy=-1, dx=-1), dict(dy=-1, dx=1))):
        clear(by, wd.at[i])

    for c in range(2):
        loads[c].wait()

        def add(z, total, c=c):
            return total + side_v[pl.ds(c * LEVEL + (z + 1) * CY, CY), :]

        t_v[pl.ds(c * CY, CY), :] = lax.fori_loop(
            0, CZ, add, jnp.zeros((CY, CX), jnp.float32), unroll=8
        )
    pl.semaphore_wait(barrier, greeted)

    layers = []
    for c in range(2):
        layers.append(
            Hop(
                side_hbm.at[pl.ds(c * CZ * CY + (CZ - 1) * CY, CY)],
                side_v.at[pl.ds(c * LEVEL, CY)],
                s_z.at[0, c],
                r_z.at[0, c],
                dz=1,
            )
        )
        layers.append(
            Hop(
                side_hbm.at[pl.ds(c * CZ * CY, 2 * CY)],
                side_v.at[pl.ds(c * LEVEL + (CZ + 1) * CY, 2 * CY)],
                s_z.at[1, c],
                r_z.at[1, c],
                dz=-1,
            )
        )
    for one in layers:
        one.start()

    ups = [
        Hop(t_v, tr.at[d - 1], s_t.at[d - 1], r_t.at[d - 1], dz=d) for d in (4, 5, 3, 6, 2, 7, 1)
    ]
    for one in ups:
        one.start()

    sums = [
        Hop(mc_s, mc_r.at[pl.ds(8 * (d - 1), 8)], s_mc.at[d - 1], r_mc.at[d - 1], dy=d)
        for d in range(1, NY_DEV)
    ] + [
        Hop(mr_s, mr_r.at[pl.ds(CY * (d - 1), CY)], s_mr.at[d - 1], r_mr.at[d - 1], dx=d)
        for d in range(1, NX_DEV)
    ]
    for one in sums:
        one.start()

    for c in range(2):
        for k in range(2):
            here = pl.ds((2 * c + k) * CZ, CZ)
            ys_lo[here, :] = side_v[pl.ds(c * LEVEL + CY + k, CZ, stride=CY), :]
            ys_hi[here, :] = side_v[pl.ds(c * LEVEL + CY + CY - 2 + k, CZ, stride=CY), :]
    faces = [
        Hop(ys_lo, yr_hi, s_y.at[0], r_y.at[0], dy=-1),
        Hop(ys_hi, yr_lo, s_y.at[1], r_y.at[1], dy=1),
    ]
    for one in faces:
        one.start()

    main_lane = lanes((CY, CX))

    def main(c, level):
        return side_v[pl.ds(pl.multiple_of(c * LEVEL + level * CY, 8), CY), :]

    def place(zi, running, packed):
        first = 2 * zi
        out = []
        for c in range(2):
            turned = pltpu.roll(running[c], first + 2, 1)
            hi, lo = packed[2 * c], packed[2 * c + 1]
            out.append(jnp.where((main_lane == first) | (main_lane == first + 1), turned, hi))
            out.append(jnp.where((main_lane == first + 2) | (main_lane == first + 3), turned, lo))
        return tuple(out)

    nothing = jnp.zeros((CY, CX), jnp.float32)

    def pack(zi, carry):
        running, packed = carry
        running = tuple(running[c] + main(c, zi - 1) for c in range(2))
        return running, place(zi, running, packed)

    running, packed = lax.fori_loop(
        2, CZ + 2, pack, ((nothing,) * 2, (nothing,) * 4), unroll=UNROLL_PACK
    )

    def slot(k, z, high):
        return pl.ds(pl.multiple_of((k * (CZ + 2) + z + 1) * high, 8), high)

    class Strip:
        def __init__(self, source, store, high):
            self.source, self.store, self.high = source, store, high

        def raw(self, c, level):
            first = pl.multiple_of((c * EZ + level) * self.high, 8)
            return spacing * self.source[pl.ds(first, self.high), :]

        def level(self, z, ax, ay, before):
            bx, by = self.raw(0, z + 2), self.raw(1, z + 2)
            bz = (turn(ay, -1, 1) - ay) - (turn(ax, -1, 0) - ax)
            values = (
                bx,
                by,
                bz,
                (bz - turn(bz, 1, 0)) - (by - before[1]),
                (bx - before[0]) - (bz - turn(bz, 1, 1)),
                (by - turn(by, 1, 1)) - (bx - turn(bx, 1, 0)),
                ax,
                ay,
            )
            for k, x in enumerate(values):
                self.store[slot(k, z, self.high), :] = x
            return ax + by, ay - bx, (bx, by)

        def middle(self, unroll):
            ground = (self.raw(0, 1), self.raw(1, 1))
            return lax.fori_loop(
                0,
                CZ - 1,
                lambda z, carry: self.level(z, *carry),
                (ground[1], -ground[0], ground),
                unroll=unroll,
            )

        def ends(self, ax, ay, before):
            level_zero = jnp.zeros((self.high, CX), jnp.float32)
            self.level(-1, level_zero, level_zero, (self.raw(0, 0), self.raw(1, 0)))
            ax, ay, before = self.level(CZ - 1, ax, ay, before)
            self.level(CZ, ax, ay, before)

        def at_the_bounds(self, qx, qy):
            pre, high = self.store, self.high

            @pl.when(gz == 0)
            def _():
                pre[slot(3, 0, high), :] = pre[slot(3, 0, high), :] + qx
                pre[slot(4, 0, high), :] = pre[slot(4, 0, high), :] + qy

            @pl.when(gz == NZ_DEV - 1)
            def _():
                z = CZ - 1
                bx, by = pre[slot(0, z, high), :], pre[slot(1, z, high), :]
                tx = pre[slot(7, z, high), :] + qy
                ty = -(pre[slot(6, z, high), :] + qx)
                pre[slot(0, z, high), :] = tx
                pre[slot(1, z, high), :] = ty
                pre[slot(3, z, high), :] = pre[slot(3, z, high), :] - (ty - by)
                pre[slot(4, z, high), :] = pre[slot(4, z, high), :] + (tx - bx)
                pre[slot(5, z, high), :] = (ty - turn(ty, 1, 1)) - (tx - turn(tx, 1, 0))

        def finish(self, z, planes_of):
            qx, qy, cz, cjx, cjy = planes_of
            bx, by, bz, jx, jy, jz, ax, ay = (
                self.store[slot(k, z, self.high), :] for k in range(8)
            )
            d = push((bx, by, bz + cz), (jx + cjx, jy + cjy, jz))
            return (ax + qx + d[0], ay + qy + d[1], d[2])

    def planes_for(qx, qy):
        cz = (turn(qy, -1, 1) - qy) - (turn(qx, -1, 0) - qx)
        return qx, qy, cz, cz - turn(cz, 1, 0), turn(cz, 1, 1) - cz

    block = Strip(side_v, pre_m, CY)
    strip = Strip(ext_v, pre_e, 8)
    block_end = block.middle(UNROLL_PRE)

    col = mag
    row_of = rows((CY, CX))
    for k in (1, 2, 4, 8, 16):
        col = col + jnp.where(row_of >= k, pltpu.roll(col, k, 0), 0.0)
    lin = mag
    lane_of = lanes((CY, CX))
    for k in (1, 2, 4, 8, 16, 32, 64):
        lin = lin + jnp.where(lane_of >= k, pltpu.roll(lin, k, 1), 0.0)
    q_v[pl.ds(0, CY), :] = col
    q_v[pl.ds(CY, CY), :] = lin
    for d, one in enumerate(sums[: NY_DEV - 1]):

        @pl.when(one.back)
        def _(d=d, one=one):
            one.wait_recv()
            q_v[pl.ds(0, CY), :] = q_v[pl.ds(0, CY), :] + mc_r[pl.ds(8 * d, 1), :]

    for d, one in enumerate(sums[NY_DEV - 1 :]):

        @pl.when(one.back)
        def _(d=d, one=one):
            one.wait_recv()
            q_v[pl.ds(CY, CY), :] = q_v[pl.ds(CY, CY), :] + mr_r[pl.ds(CY * d, CY), :]

    q_v[pl.ds(0, CY), :] = (-0.5 * spacing) * q_v[pl.ds(0, CY), :]
    q_v[pl.ds(CY, CY), :] = (0.5 * spacing) * q_v[pl.ds(CY, CY), :]

    for one in faces:
        one.wait_recv()
    for c in range(2):
        for k in range(2):
            here = pl.ds((2 * c + k) * CZ, CZ)
            for j, ref in enumerate((ys_hi, yr_hi, yr_lo, ys_lo)):
                ext_v[pl.ds((c * EZ + 1) * 8 + 2 * j + k, CZ, stride=8), :] = ref[here, :]

    strip_end = strip.middle(UNROLL_STRIP)

    for one in layers:
        one.wait_recv()
    for zi in (CZ + 2, CZ + 3):
        running, packed = pack(zi, (running, packed))
    packed = place(0, tuple(-main(c, 0) for c in range(2)), packed)

    for c in range(2):
        for i, level in enumerate((0, CZ + 1, CZ + 2)):
            first = c * LEVEL + level * CY
            to = (c * 3 + i) * 2
            cs_lo[pl.ds(to, 2), :] = side_v[pl.ds(first, 2), :]
            cs_hi[pl.ds(to, 2), :] = side_v[pl.ds(first + CY - 2, 2), :]
    cs_lo[pl.ds(12, 4), :] = jnp.zeros((4, CX), jnp.float32)
    cs_hi[pl.ds(12, 4), :] = jnp.zeros((4, CX), jnp.float32)
    corners = [
        Hop(cs_lo, cr_hi, s_c.at[0], r_c.at[0], dy=-1),
        Hop(cs_hi, cr_lo, s_c.at[1], r_c.at[1], dy=1),
    ]
    for one in corners:
        one.start()

    block.ends(*block_end)

    for one in ups:

        @pl.when(one.back)
        def _(one=one):
            one.wait_recv()

    for d in range(1, NZ_DEV):

        @pl.when(there(dz=-d))
        def _(d=d):
            q_v[pl.ds(0, CY), :] = q_v[pl.ds(0, CY), :] + spacing * tr[d - 1, pl.ds(CY, CY), :]
            q_v[pl.ds(CY, CY), :] = q_v[pl.ds(CY, CY), :] - spacing * tr[d - 1, pl.ds(0, CY), :]

    q = tuple(q_v[pl.ds(c * CY, CY), :] for c in range(2))
    def spread(x, i):
        return jnp.broadcast_to(x[:, i : i + 1], x.shape)

    main_even = main_lane % 2 == 0
    for c in range(2):
        o, sign = (1, spacing) if c == 0 else (0, -spacing)
        hi = jnp.where(main_even, spread(q[c], CX - 2), spread(q[c], CX - 1))
        lo = jnp.where(main_even, spread(q[c], 0), spread(q[c], 1))
        hi, lo = hi + sign * packed[2 * o], lo + sign * packed[2 * o + 1]
        for k, (ref, x) in enumerate(((w_hi, hi), (w_lo, lo))):
            ref[pl.ds(c * CY, CY), :] = x
            wt_lo[pl.ds((2 * k + c) * 8, 8), :] = x[:8]
            wt_hi[pl.ds((2 * k + c) * 8, 8), :] = x[CY - 8 :]
        qt_lo[pl.ds(c * 8, 8), :] = q[c][:8]
        qt_hi[pl.ds(c * 8, 8), :] = q[c][CY - 8 :]
    columns = [
        Hop(w_hi, wn_lo, s_w.at[0], r_w.at[0], dx=1),
        Hop(w_lo, wn_hi, s_w.at[1], r_w.at[1], dx=-1),
        Hop(wt_lo.at[pl.ds(0, 16)], wd.at[0], s_w.at[4], r_w.at[4], dy=-1, dx=1),
        Hop(wt_lo.at[pl.ds(16, 16)], wd.at[1], s_w.at[5], r_w.at[5], dy=-1, dx=-1),
        Hop(wt_hi.at[pl.ds(0, 16)], wd.at[2], s_w.at[6], r_w.at[6], dy=1, dx=1),
        Hop(wt_hi.at[pl.ds(16, 16)], wd.at[3], s_w.at[7], r_w.at[7], dy=1, dx=-1),
        Hop(wt_lo, wy_hi, s_w.at[2], r_w.at[2], dy=-1),
        Hop(wt_hi, wy_lo, s_w.at[3], r_w.at[3], dy=1),
        Hop(qt_lo, qy_hi, s_q.at[0], r_q.at[0], dy=-1),
        Hop(qt_hi, qy_lo, s_q.at[1], r_q.at[1], dy=1),
    ]
    for one in columns:
        one.start()

    block.at_the_bounds(*q)
    block_planes = planes_for(*q)

    def finish_block(z, _):
        new = block.finish(z, block_planes)
        for c in range(3):
            first = pl.multiple_of((c * (CZ + 2) + z + 1) * EY, 8)
            a1_out[pl.ds(first, CY), :] = new[c]
        return 0

    lax.fori_loop(-1, CZ + 1, finish_block, 0, unroll=UNROLL_POST)

    for one in corners:
        one.wait_recv()
    for c in range(2):
        for i, level in enumerate((0, CZ + 1, CZ + 2)):
            first = (c * EZ + level) * 8
            of = pl.ds((c * 3 + i) * 2, 2)
            for j, ref in enumerate((cs_hi, cr_hi, cr_lo, cs_lo)):
                ext_v[pl.ds(first + 2 * j, 2), :] = ref[of, :]
    strip.ends(*strip_end)

    row8 = rows((8, CX))

    def plane(middle, from_hi, from_lo):
        tile = jnp.where(row8 < 2, from_hi, jnp.where(row8 >= 6, from_lo, 0.0))
        return jnp.concatenate([middle, tile], axis=0)

    for one in columns:
        one.wait_recv()
    lane, row = lanes((EY, CX)), rows((EY, CX))
    even = lane % 2 == 0
    level_ok = ((lane >= 4) | (gz > 0)) & ((lane < 2 * (CZ + 2)) | (gz < NZ_DEV - 1))
    ea = [[None, None] for _ in range(4)]
    carry_plane = []
    for c in range(2):
        mine, tile, other = pl.ds(c * CY, CY), pl.ds(c * 8, 8), pl.ds(16 + c * 8, 8)
        hi = plane(w_hi[mine, :], wy_hi[tile, :], wy_lo[tile, :])
        lo = plane(w_lo[mine, :], wy_hi[other, :], wy_lo[other, :])
        lon = plane(wn_lo[mine, :], wd[0, tile, :], wd[2, tile, :])
        hin = plane(wn_hi[mine, :], wd[1, tile, :], wd[3, tile, :])
        pairs = (
            (hi, turn(lon, 1, 1)),
            (turn(hi, -1, 1), lon),
            (turn(hin, -2, 1), turn(lo, -1, 1)),
            (turn(hin, -3, 1), turn(lo, -2, 1)),
        )
        for m, pair in enumerate(pairs):
            ea[m][c] = jnp.where(level_ok, jnp.where(even, *pair), 0.0)
        around = (q[c][CY - 8 :], qy_hi[tile, :], qy_lo[tile, :], q[c][:8])
        turned = [turn(x, by, 0) for x, by in zip(around, (2, 2, -2, -2))]
        carry_plane.append(
            jnp.where(
                row8 < 4,
                jnp.where(row8 < 2, turned[0], turned[1]),
                jnp.where(row8 < 6, turned[2], turned[3]),
            )
        )

    row_ok = ((row < CY) | (row >= CY + 2) | (gy < NY_DEV - 1)) & ((row < CY + 2) | (gy > 0))
    eb = []
    for m in range(3):
        up_y = (turn(ea[m][0], -1, 0),)
        up_z = tuple(turn(x, -2, 1) for x in ea[m])
        eb.append(fields(ea[m], up_z, up_y, ea[m + 1], True))
    ea1 = []
    for m in (1, 2):
        down_z = tuple(turn(x, 2, 1) for x in eb[m])
        down_y = tuple(turn(x, 1, 0) for x in eb[m])
        d = drive(eb[m], down_z, down_y, eb[m - 1])
        if m == 1:
            outside = (lane % 2 == 1) & (gx == 0)
        else:
            outside = (lane % 2 == 0) & (gx == NX_DEV - 1)
        ok = row_ok & jnp.logical_not(outside) & level_ok
        a = (ea[m][0] + d[0], ea[m][1] + d[1], d[2])
        ea1.append(tuple(jnp.where(ok, x, 0.0) for x in a))
    near = ea1[0]
    eb1 = fields(
        near,
        tuple(turn(x, -2, 1) for x in near),
        tuple(turn(x, -1, 0) for x in near),
        ea1[1],
        False,
    )
    v_out[pl.ds(0, EY), :] = jnp.where(even, ea1[1][1], eb1[2])
    v_out[pl.ds(EY, EY), :] = jnp.where(even, ea1[1][2], eb1[1])
    edge = tuple(jnp.where(even, ea1[0][c], ea1[1][c]) for c in range(3))

    strip.at_the_bounds(*carry_plane)
    strip_planes = planes_for(*carry_plane)
    rim = (lane == 0) | (lane == CX - 1)
    tile_ok = ((row8 >= 2) | (gy < NY_DEV - 1)) & ((row8 < 2) | (gy > 0))

    def finish_strip(z, _):
        new = strip.finish(z, strip_planes)
        shift = lax.rem(2 * CX - 1 - 2 * (z + 2), CX)
        for c in range(3):
            first = pl.multiple_of((c * (CZ + 2) + z + 1) * EY, 8)
            left, right = turn(new[c], -2, 0), turn(new[c], 2, 0)
            x = jnp.concatenate(
                [
                    jnp.where(row8 == 0, right, a1_out[pl.ds(first, 8), :]),
                    a1_out[pl.ds(first + 8, 16), :],
                    jnp.where(row8 == 7, left, a1_out[pl.ds(first + 24, 8), :]),
                    jnp.where(row8 < 4, left, right),
                ],
                axis=0,
            )
            x = jnp.where(rim, pltpu.roll(edge[c], shift, 1), x)
            a1_out[pl.ds(first, CY), :] = x[:CY]
            a1_out[pl.ds(first + CY, 8), :] = jnp.where(tile_ok, x[CY:], 0.0)
        return 0

    lax.fori_loop(-1, CZ + 1, finish_strip, 0, unroll=UNROLL_EDGE)

    @pl.when(gz == 0)
    def _():
        for c in range(3):
            a1_out[slot(c, -1, EY), :] = jnp.zeros((EY, CX), jnp.float32)

    @pl.when(gz == NZ_DEV - 1)
    def _():
        for c in range(3):
            a1_out[slot(c, CZ, EY), :] = jnp.zeros((EY, CX), jnp.float32)

    for one in ups + sums + layers + faces + corners + columns:
        one.wait_send()


def step_kernel(a1, v_ref, out_hbm, out_v, store_sem):
    lane = lanes((EY, CX))
    first_lane, last_lane = lane == 0, lane == CX - 1

    def new_at(z):
        return tuple(
            a1[pl.ds(pl.multiple_of((c * (CZ + 2) + z + 1) * EY, 8), EY), :] for c in range(3)
        )

    def beside(z):
        shift = lax.rem(2 * CX - 1 - 2 * (z + 2), CX)
        return tuple(pltpu.roll(v_ref[pl.ds(k * EY, EY), :], shift, 1) for k in range(2))

    def second_field(a, a_up, v):
        yp = (turn(a[0], -1, 0), None, turn(a[2], -1, 0))
        xp = (
            None,
            jnp.where(last_lane, v[0], turn(a[1], -1, 1)),
            jnp.where(last_lane, v[1], turn(a[2], -1, 1)),
        )
        return fields(a, a_up, yp, xp, False)

    first_main, main = first_lane[:CY], slice(0, CY)

    def level_two(z, carry):
        a, before = carry
        v = beside(z)
        a_up = new_at(z + 1)
        b = second_field(a, a_up, v)
        ym = (turn(b[0], 1, 0)[main], None, turn(b[2], 1, 0)[main])
        own = tuple(x[main] for x in b)
        xm = (
            None,
            jnp.where(first_main, v[1][main], turn(own[1], 1, 1)),
            jnp.where(first_main, v[0][main], turn(own[2], 1, 1)),
        )
        d = drive(own, before, ym, xm)
        for c in range(3):
            out_v[pl.ds(pl.multiple_of((c * CZ + z) * CY, 8), CY), :] = a[c][main] + d[c]
        return a_up, (own[0], own[1])

    below, a = new_at(-1), new_at(0)
    b = second_field(below, a, beside(-1))
    carry = (a, (b[0][main], b[1][main]))
    part = 8

    def store(k, c):
        there = pl.ds(pl.multiple_of((c * CZ + k * part) * CY, 8), part * CY)
        return pltpu.make_async_copy(out_v.at[there], out_hbm.at[there], store_sem.at[k, c])

    def chunk(k, carry):
        carry = lax.fori_loop(
            0, part, lambda i, x: level_two(k * part + i, x), carry, unroll=4
        )
        for c in range(3):
            store(k, c).start()
        return carry

    lax.fori_loop(0, CZ // part, chunk, carry)
    for k in range(CZ // part):
        for c in range(3):
            store(k, c).wait()


def f32(*shape):
    return jax.ShapeDtypeStruct(shape, jnp.float32)


def vmem(*shape):
    return pltpu.VMEM(shape, jnp.float32)


def local(side_field, magnetogram):
    side = pltpu.with_memory_space_constraint(side_field.reshape(2 * CZ * CY, CX), pltpu.HBM)
    magnetogram = pltpu.with_memory_space_constraint(magnetogram, pltpu.HBM)
    whole = pl.BlockSpec(memory_space=pltpu.VMEM)
    dma = pltpu.SemaphoreType.DMA
    a1, v = pl.pallas_call(
        comm_kernel,
        out_shape=(f32(3 * (CZ + 2) * EY, CX), f32(2 * EY, CX)),
        in_specs=[pl.BlockSpec(memory_space=pltpu.HBM), whole],
        out_specs=(whole,) * 2,
        scratch_shapes=[
            vmem(2 * EZ * 8, CX),
            vmem(8 * (CZ + 2) * CY, CX),
            vmem(8 * (CZ + 2) * 8, CX),
            vmem(2 * LEVEL, CX),
            vmem(2 * CY, CX),
            vmem(NZ_DEV - 1, 2 * CY, CX),
        ]
        + [vmem(4 * CZ, CX)] * 4
        + [vmem(16, CX)] * 4
        + [vmem(2 * CY, CX)] * 4
        + [vmem(32, CX)] * 4
        + [
            vmem(4, 16, CX),
            vmem(8, CX),
            vmem(CY, CX),
            vmem(8 * (NY_DEV - 1), CX),
            vmem(CY * (NX_DEV - 1), CX),
            vmem(2 * CY, CX),
            vmem(16, CX),
            vmem(16, CX),
            vmem(16, CX),
            vmem(16, CX),
        ]
        + [dma((2,))]
        + [dma((NZ_DEV - 1,))] * 2
        + [dma((2, 2))] * 2
        + [dma((2,))] * 4
        + [dma((8,))] * 2
        + [dma((NY_DEV - 1,))] * 2
        + [dma((NX_DEV - 1,))] * 2
        + [dma((2,))] * 2,
        compiler_params=pltpu.CompilerParams(
            collective_id=0, has_side_effects=True, vmem_limit_bytes=VMEM_BYTES
        ),
        name="exchange",
    )(side, magnetogram)
    out = pl.pallas_call(
        step_kernel,
        out_shape=f32(3 * CZ * CY, CX),
        in_specs=[whole] * 2,
        out_specs=pl.BlockSpec(memory_space=pltpu.HBM),
        scratch_shapes=[vmem(3 * CZ * CY, CX), dma((CZ // 8, 3))],
        compiler_params=pltpu.CompilerParams(vmem_limit_bytes=VMEM_BYTES),
        name="steps",
    )(a1, v)
    return out.reshape(3, CZ, CY, CX)


def solution(mesh):
    return jax.shard_map(
        local,
        mesh=mesh,
        in_specs=(P(None, "gz", "gy", "gx"), P("gy", "gx")),
        out_specs=P(None, "gz", "gy", "gx"),
        check_vma=False,
    )
```

time: 31.7 us -> 25.5 us (0.80)
  Pallas kernels: 31.5 us -> 25.4 us
    pallas_call x2, Pallas kernels: 31.5 us -> 25.4 us  [the longest x1 21.5 us: local(): pl.pallas_call(comm_kernel, out_shape=(f32(3 * (CZ + 2) * EY, CX), f32(2...]
where the time goes in v3:
time: 25.5 us; the launch traced here: 25.4 us
  Pallas kernels  25.4 us (100%)
    pallas_call x1, Pallas kernels, local(): pl.pallas_call(comm_kernel, out_shape=(f32(3 * (CZ + 2) * EY, CX), f32(2...  21.5 us
    pallas_call x1, Pallas kernels, local(): pl.pallas_call(step_kernel, out_shape=f32(3 * CZ * CY, CX), in_specs=[who...  3.87 us

profile of v3, /device:TPU:1, one launch (start us, length us, event | category | flops | bytes accessed | tf_op | source)
XLA Modules:
  0.0 25.4 jit_solution(5753496256007457142)
XLA Ops:
  0.0 21.5 %exchange.1 = (f32[6000,128]{1,0:T(8,128)S(1)}, f32[80,128]{1,0:T(8,128)S(1)}) custom-call(f32[3072,128]{1,0:T(8,128)} %bitcast.2, f32[32,128]{1,0:T(8,128)} %mag_ref.1), custom_call_target="tpu_custom_call" | custom-call | tf_op jit(solution)/shard_map/exchange/pallas_call | solution.py:691
  21.5 3.9 %steps.1 = f32[4608,128]{1,0:T(8,128)} custom-call(f32[6000,128]{1,0:T(8,128)S(1)} %get-tuple-element.7.a1, f32[80,128]{1,0:T(8,128)S(1)} %get-tuple-element.8.v_ref), custom_call_target="tpu_custom_call" | custom-call | tf_op jit(solution)/shard_map/steps/pallas_call | solution.py:733

commit v4 on v3

--- a/solution.py
+++ b/solution.py
@@ -99,6 +99,9 @@
     qt_hi,
     qy_lo,
     qy_hi,
+    here_sem,
+    wide,
+    far,
     load_sem,
     s_t,
     r_t,
@@ -170,21 +173,47 @@
     for load in loads:
         load.start()
 
+    half = NZ_DEV // 2
+    place_z = lax.rem(gz, half)
+    middle = (gz == half - 1).astype(jnp.int32)
     barrier = pltpu.get_barrier_semaphore()
-    for peer in (
-        [at(dz=d) for d in range(1, NZ_DEV)]
-        + [at(dy=d) for d in range(1, NY_DEV)]
-        + [at(dx=d) for d in range(1, NX_DEV)]
-    ):
-        pl.semaphore_signal(barrier, inc=1, device_id=peer, device_id_type=MESH)
-    diagonal = [dict(dy=a, dx=b) for a in (1, -1) for b in (1, -1)]
-    greeted = jnp.int32(NZ_DEV + NY_DEV + NX_DEV - 3)
-    for by in diagonal:
-        greeted = greeted + there(**by).astype(jnp.int32)
-
-        @pl.when(there(**by))
-        def _(by=by):
-            pl.semaphore_signal(barrier, inc=1, device_id=at(**by), device_id_type=MESH)
+
+    def tell(sem, ok, **by):
+        @pl.when(ok)
+        def _():
+            pl.semaphore_signal(sem, inc=1, device_id=at(**by), device_id_type=MESH)
+
+    def wait_for(sem, count):
+        @pl.when(count > 0)
+        def _():
+            pl.semaphore_wait(sem, count)
+
+    def close(d):
+        return jnp.logical_or(place_z >= d, jnp.logical_and(gz == half, d == 1))
+
+    higher = (
+        [dict(dz=d) for d in range(1, NZ_DEV)]
+        + [dict(dy=d) for d in range(1, NY_DEV)]
+        + [dict(dx=d) for d in range(1, NX_DEV)]
+        + [dict(dy=1, dx=1), dict(dy=1, dx=-1)]
+    )
+    heard, answers = gz + gy + gx, (half - 1 - place_z) + middle
+    answers = answers + there(dy=1).astype(jnp.int32) + there(dx=1).astype(jnp.int32)
+    others = jnp.maximum(NY_DEV - 2 - gy, 0) + jnp.maximum(NX_DEV - 2 - gx, 0)
+    for by in higher:
+        tell(barrier, there(**by), **by)
+    for by in higher[-2:]:
+        heard = heard + there(**{k: -v for k, v in by.items()}).astype(jnp.int32)
+        answers = answers + there(**by).astype(jnp.int32)
+    wait_for(barrier, heard)
+    for by in higher:
+        back = {k: -v for k, v in by.items()}
+        if "dz" in by:
+            tell(here_sem, there(**back) & close(by["dz"]), **back)
+            tell(far, there(**back) & jnp.logical_not(close(by["dz"])), **back)
+        else:
+            step = max(by.values())
+            tell(here_sem if step == 1 else wide, there(**back), **back)
 
     mag = mag_ref[...]
     mc_s[...] = jnp.broadcast_to(jnp.sum(mag, axis=0, keepdims=True), (8, CX))
@@ -218,7 +247,8 @@
         t_v[pl.ds(c * CY, CY), :] = lax.fori_loop(
             0, CZ, add, jnp.zeros((CY, CX), jnp.float32), unroll=8
         )
-    pl.semaphore_wait(barrier, greeted)
+
+    wait_for(here_sem, answers)
 
     layers = []
     for c in range(2):
@@ -244,10 +274,14 @@
         one.start()
 
     ups = [
-        Hop(t_v, tr.at[d - 1], s_t.at[d - 1], r_t.at[d - 1], dz=d) for d in (4, 5, 3, 6, 2, 7, 1)
+        Hop(t_v, tr.at[d - 1], s_t.at[d - 1], r_t.at[d - 1], dz=d) for d in range(1, NZ_DEV)
     ]
-    for one in ups:
-        one.start()
+
+    def near(d):
+        return jnp.logical_or(place_z + d < half, jnp.logical_and(gz == half - 1, d == 1))
+
+    for d, one in enumerate(ups, 1):
+        pl.when(one.to & near(d))(one.copy.start)
 
     sums = [
         Hop(mc_s, mc_r.at[pl.ds(8 * (d - 1), 8)], s_mc.at[d - 1], r_mc.at[d - 1], dy=d)
@@ -256,8 +290,6 @@
         Hop(mr_s, mr_r.at[pl.ds(CY * (d - 1), CY)], s_mr.at[d - 1], r_mr.at[d - 1], dx=d)
         for d in range(1, NX_DEV)
     ]
-    for one in sums:
-        one.start()
 
     for c in range(2):
         for k in range(2):
@@ -296,6 +328,17 @@
     running, packed = lax.fori_loop(
         2, CZ + 2, pack, ((nothing,) * 2, (nothing,) * 4), unroll=UNROLL_PACK
     )
+
+    wait_for(wide, others)
+    for one in sums:
+        one.start()
+
+    @pl.when(gz < half)
+    def _():
+        pl.semaphore_wait(far, half - middle)
+
+    for d, one in enumerate(ups, 1):
+        pl.when(one.to & jnp.logical_not(near(d)))(one.copy.start)
 
     def slot(k, z, high):
         return pl.ds(pl.multiple_of((k * (CZ + 2) + z + 1) * high, 8), high)
@@ -403,16 +446,6 @@
 
     q_v[pl.ds(0, CY), :] = (-0.5 * spacing) * q_v[pl.ds(0, CY), :]
     q_v[pl.ds(CY, CY), :] = (0.5 * spacing) * q_v[pl.ds(CY, CY), :]
-
-    for one in faces:
-        one.wait_recv()
-    for c in range(2):
-        for k in range(2):
-            here = pl.ds((2 * c + k) * CZ, CZ)
-            for j, ref in enumerate((ys_hi, yr_hi, yr_lo, ys_lo)):
-                ext_v[pl.ds((c * EZ + 1) * 8 + 2 * j + k, CZ, stride=8), :] = ref[here, :]
-
-    strip_end = strip.middle(UNROLL_STRIP)
 
     for one in layers:
         one.wait_recv()
@@ -493,6 +526,14 @@
 
     lax.fori_loop(-1, CZ + 1, finish_block, 0, unroll=UNROLL_POST)
 
+    for one in faces:
+        one.wait_recv()
+    for c in range(2):
+        for k in range(2):
+            here = pl.ds((2 * c + k) * CZ, CZ)
+            for j, ref in enumerate((ys_hi, yr_hi, yr_lo, ys_lo)):
+                ext_v[pl.ds((c * EZ + 1) * 8 + 2 * j + k, CZ, stride=8), :] = ref[here, :]
+
     for one in corners:
         one.wait_recv()
     for c in range(2):
@@ -501,7 +542,7 @@
             of = pl.ds((c * 3 + i) * 2, 2)
             for j, ref in enumerate((cs_hi, cr_hi, cr_lo, cs_lo)):
                 ext_v[pl.ds(first + 2 * j, 2), :] = ref[of, :]
-    strip.ends(*strip_end)
+    strip.ends(*strip.middle(UNROLL_STRIP))
 
     row8 = rows((8, CX))
 
@@ -717,6 +758,7 @@
             vmem(16, CX),
             vmem(16, CX),
         ]
+        + [pltpu.SemaphoreType.REGULAR] * 3
         + [dma((2,))]
         + [dma((NZ_DEV - 1,))] * 2
         + [dma((2, 2))] * 2

time: 25.5 us -> 24.4 us (0.957)
  the two profiles are of different devices: /device:TPU:1 before, /device:TPU:193 now
where the time goes in v4:
time: 24.4 us; the launch traced here: 24.2 us
  Pallas kernels  24.2 us (99%)
    pallas_call x1, Pallas kernels, local(): pl.pallas_call(comm_kernel, out_shape=(f32(3 * (CZ + 2) * EY, CX), f32(2...  20.4 us
    pallas_call x1, Pallas kernels, local(): pl.pallas_call(step_kernel, out_shape=f32(3 * CZ * CY, CX), in_specs=[who...  3.87 us

profile of v4, /device:TPU:193, one launch (start us, length us, event | category | flops | bytes accessed | tf_op | source)
XLA Modules:
  0.0 24.2 jit_solution(6196455003973830140)
XLA Ops:
  0.0 20.4 %exchange.1 = (f32[6000,128]{1,0:T(8,128)S(1)}, f32[80,128]{1,0:T(8,128)S(1)}) custom-call(f32[3072,128]{1,0:T(8,128)} %bitcast.2, f32[32,128]{1,0:T(8,128)} %mag_ref.1), custom_call_target="tpu_custom_call" | custom-call | tf_op jit(solution)/shard_map/exchange/pallas_call | solution.py:732
  20.4 3.9 %steps.1 = f32[4608,128]{1,0:T(8,128)} custom-call(f32[6000,128]{1,0:T(8,128)S(1)} %get-tuple-element.7.a1, f32[80,128]{1,0:T(8,128)S(1)} %get-tuple-element.8.v_ref), custom_call_target="tpu_custom_call" | custom-call | tf_op jit(solution)/shard_map/steps/pallas_call | solution.py:775

commit v5 on v4

--- a/solution.py
+++ b/solution.py
@@ -64,9 +64,10 @@
 
 def comm_kernel(
     side_hbm,
-    mag_ref,
+    mag_hbm,
     a1_out,
     v_out,
+    mag_ref,
     ext_v,
     pre_m,
     pre_e,
@@ -95,6 +96,8 @@
     mc_r,
     mr_r,
     q_v,
+    qc,
+    qn,
     qt_lo,
     qt_hi,
     qy_lo,
@@ -162,17 +165,6 @@
         def wait_recv(self):
             pl.when(self.back)(self.copy.wait_recv)
 
-    loads = [
-        pltpu.make_async_copy(
-            side_hbm.at[pl.ds(c * CZ * CY, CZ * CY)],
-            side_v.at[pl.ds(c * LEVEL + CY, CZ * CY)],
-            load_sem.at[c],
-        )
-        for c in range(2)
-    ]
-    for load in loads:
-        load.start()
-
     half = NZ_DEV // 2
     place_z = lax.rem(gz, half)
     middle = (gz == half - 1).astype(jnp.int32)
@@ -205,6 +197,19 @@
     for by in higher[-2:]:
         heard = heard + there(**{k: -v for k, v in by.items()}).astype(jnp.int32)
         answers = answers + there(**by).astype(jnp.int32)
+    part = CZ // 2 * CY
+    loads = [
+        pltpu.make_async_copy(
+            side_hbm.at[pl.ds(c * CZ * CY + k * part, part)],
+            side_v.at[pl.ds(c * LEVEL + CY + k * part, part)],
+            load_sem.at[2 * c + k],
+        )
+        for c in range(2)
+        for k in range(2)
+    ]
+    loads.append(pltpu.make_async_copy(mag_hbm, mag_ref, load_sem.at[4]))
+    for load in loads:
+        load.start()
     wait_for(barrier, heard)
     for by in higher:
         back = {k: -v for k, v in by.items()}
@@ -214,10 +219,6 @@
         else:
             step = max(by.values())
             tell(here_sem if step == 1 else wide, there(**back), **back)
-
-    mag = mag_ref[...]
-    mc_s[...] = jnp.broadcast_to(jnp.sum(mag, axis=0, keepdims=True), (8, CX))
-    mr_s[...] = jnp.broadcast_to(jnp.sum(mag, axis=1, keepdims=True), (CY, CX))
 
     def clear(by, *refs):
         @pl.when(jnp.logical_not(there(**by)))
@@ -235,19 +236,21 @@
     clear(dict(dy=1), yr_hi, cr_hi, wy_hi, qy_hi)
     clear(dict(dx=-1), wn_lo)
     clear(dict(dx=1), wn_hi)
+    clear(dict(dx=-1), qn.at[0])
+    clear(dict(dx=1), qn.at[1])
     for i, by in enumerate((dict(dy=1, dx=-1), dict(dy=1, dx=1), dict(dy=-1, dx=-1), dict(dy=-1, dx=1))):
-        clear(by, wd.at[i])
-
-    for c in range(2):
-        loads[c].wait()
-
-        def add(z, total, c=c):
-            return total + side_v[pl.ds(c * LEVEL + (z + 1) * CY, CY), :]
-
-        t_v[pl.ds(c * CY, CY), :] = lax.fori_loop(
-            0, CZ, add, jnp.zeros((CY, CX), jnp.float32), unroll=8
-        )
-
+        clear(by, wd.at[i], qn.at[2 + i])
+
+    for c in range(2):
+        total = jnp.zeros((CY, CX), jnp.float32)
+        for k in range(2):
+            loads[2 * c + k].wait()
+
+            def add(z, total, c=c):
+                return total + side_v[pl.ds(c * LEVEL + (z + 1) * CY, CY), :]
+
+            total = lax.fori_loop(k * CZ // 2, (k + 1) * CZ // 2, add, total, unroll=8)
+        t_v[pl.ds(c * CY, CY), :] = total
     wait_for(here_sem, answers)
 
     layers = []
@@ -328,6 +331,11 @@
     running, packed = lax.fori_loop(
         2, CZ + 2, pack, ((nothing,) * 2, (nothing,) * 4), unroll=UNROLL_PACK
     )
+
+    loads[4].wait()
+    mag = mag_ref[...]
+    mc_s[...] = jnp.broadcast_to(jnp.sum(mag, axis=0, keepdims=True), (8, CX))
+    mr_s[...] = jnp.broadcast_to(jnp.sum(mag, axis=1, keepdims=True), (CY, CX))
 
     wait_for(wide, others)
     for one in sums:
@@ -452,6 +460,25 @@
     for zi in (CZ + 2, CZ + 3):
         running, packed = pack(zi, (running, packed))
     packed = place(0, tuple(-main(c, 0) for c in range(2)), packed)
+    for c in range(2):
+        o, sign = (1, spacing) if c == 0 else (0, -spacing)
+        for k, (ref, x) in enumerate(((w_hi, packed[2 * o]), (w_lo, packed[2 * o + 1]))):
+            x = sign * x
+            ref[pl.ds(c * CY, CY), :] = x
+            wt_lo[pl.ds((2 * k + c) * 8, 8), :] = x[:8]
+            wt_hi[pl.ds((2 * k + c) * 8, 8), :] = x[CY - 8 :]
+    columns = [
+        Hop(w_hi, wn_lo, s_w.at[0], r_w.at[0], dx=1),
+        Hop(w_lo, wn_hi, s_w.at[1], r_w.at[1], dx=-1),
+        Hop(wt_lo.at[pl.ds(0, 16)], wd.at[0], s_w.at[4], r_w.at[4], dy=-1, dx=1),
+        Hop(wt_lo.at[pl.ds(16, 16)], wd.at[1], s_w.at[5], r_w.at[5], dy=-1, dx=-1),
+        Hop(wt_hi.at[pl.ds(0, 16)], wd.at[2], s_w.at[6], r_w.at[6], dy=1, dx=1),
+        Hop(wt_hi.at[pl.ds(16, 16)], wd.at[3], s_w.at[7], r_w.at[7], dy=1, dx=-1),
+        Hop(wt_lo, wy_hi, s_w.at[2], r_w.at[2], dy=-1),
+        Hop(wt_hi, wy_lo, s_w.at[3], r_w.at[3], dy=1),
+    ]
+    for one in columns:
+        one.start()
 
     for c in range(2):
         for i, level in enumerate((0, CZ + 1, CZ + 2)):
@@ -484,34 +511,27 @@
             q_v[pl.ds(CY, CY), :] = q_v[pl.ds(CY, CY), :] - spacing * tr[d - 1, pl.ds(0, CY), :]
 
     q = tuple(q_v[pl.ds(c * CY, CY), :] for c in range(2))
-    def spread(x, i):
-        return jnp.broadcast_to(x[:, i : i + 1], x.shape)
-
-    main_even = main_lane % 2 == 0
-    for c in range(2):
-        o, sign = (1, spacing) if c == 0 else (0, -spacing)
-        hi = jnp.where(main_even, spread(q[c], CX - 2), spread(q[c], CX - 1))
-        lo = jnp.where(main_even, spread(q[c], 0), spread(q[c], 1))
-        hi, lo = hi + sign * packed[2 * o], lo + sign * packed[2 * o + 1]
-        for k, (ref, x) in enumerate(((w_hi, hi), (w_lo, lo))):
-            ref[pl.ds(c * CY, CY), :] = x
-            wt_lo[pl.ds((2 * k + c) * 8, 8), :] = x[:8]
-            wt_hi[pl.ds((2 * k + c) * 8, 8), :] = x[CY - 8 :]
+    lane8 = lanes((8, CX))
+    few = jnp.zeros((8, CX), jnp.float32)
+    for c in range(2):
+        for t in range(CY // 8):
+            first = 4 * (CY // 8 * c + t)
+            here = (lane8 >= first) & (lane8 < first + 4)
+            few = jnp.where(here, turn(q[c][8 * t : 8 * t + 8], first + 2, 1), few)
         qt_lo[pl.ds(c * 8, 8), :] = q[c][:8]
         qt_hi[pl.ds(c * 8, 8), :] = q[c][CY - 8 :]
-    columns = [
-        Hop(w_hi, wn_lo, s_w.at[0], r_w.at[0], dx=1),
-        Hop(w_lo, wn_hi, s_w.at[1], r_w.at[1], dx=-1),
-        Hop(wt_lo.at[pl.ds(0, 16)], wd.at[0], s_w.at[4], r_w.at[4], dy=-1, dx=1),
-        Hop(wt_lo.at[pl.ds(16, 16)], wd.at[1], s_w.at[5], r_w.at[5], dy=-1, dx=-1),
-        Hop(wt_hi.at[pl.ds(0, 16)], wd.at[2], s_w.at[6], r_w.at[6], dy=1, dx=1),
-        Hop(wt_hi.at[pl.ds(16, 16)], wd.at[3], s_w.at[7], r_w.at[7], dy=1, dx=-1),
-        Hop(wt_lo, wy_hi, s_w.at[2], r_w.at[2], dy=-1),
-        Hop(wt_hi, wy_lo, s_w.at[3], r_w.at[3], dy=1),
-        Hop(qt_lo, qy_hi, s_q.at[0], r_q.at[0], dy=-1),
-        Hop(qt_hi, qy_lo, s_q.at[1], r_q.at[1], dy=1),
+    qc[...] = few
+    planes = [
+        Hop(qc, qn.at[0], s_q.at[0], r_q.at[0], dx=1),
+        Hop(qc, qn.at[1], s_q.at[1], r_q.at[1], dx=-1),
+        Hop(qc, qn.at[2], s_q.at[2], r_q.at[2], dy=-1, dx=1),
+        Hop(qc, qn.at[3], s_q.at[3], r_q.at[3], dy=-1, dx=-1),
+        Hop(qc, qn.at[4], s_q.at[4], r_q.at[4], dy=1, dx=1),
+        Hop(qc, qn.at[5], s_q.at[5], r_q.at[5], dy=1, dx=-1),
+        Hop(qt_lo, qy_hi, s_q.at[6], r_q.at[6], dy=-1),
+        Hop(qt_hi, qy_lo, s_q.at[7], r_q.at[7], dy=1),
     ]
-    for one in columns:
+    for one in planes:
         one.start()
 
     block.at_the_bounds(*q)
@@ -555,8 +575,7 @@
     lane, row = lanes((EY, CX)), rows((EY, CX))
     even = lane % 2 == 0
     level_ok = ((lane >= 4) | (gz > 0)) & ((lane < 2 * (CZ + 2)) | (gz < NZ_DEV - 1))
-    ea = [[None, None] for _ in range(4)]
-    carry_plane = []
+    grown = []
     for c in range(2):
         mine, tile, other = pl.ds(c * CY, CY), pl.ds(c * 8, 8), pl.ds(16 + c * 8, 8)
         hi = plane(w_hi[mine, :], wy_hi[tile, :], wy_lo[tile, :])
@@ -569,8 +588,35 @@
             (turn(hin, -2, 1), turn(lo, -1, 1)),
             (turn(hin, -3, 1), turn(lo, -2, 1)),
         )
-        for m, pair in enumerate(pairs):
-            ea[m][c] = jnp.where(level_ok, jnp.where(even, *pair), 0.0)
+        grown.append([jnp.where(even, *pair) for pair in pairs])
+
+    for one in planes:
+        one.wait_recv()
+
+    def spread(x, i):
+        return jnp.broadcast_to(x[:, i : i + 1], x.shape)
+
+    def beyond(side, from_hi, from_lo, c, i):
+        first = 4 * (CY // 8) * c + i
+        x, x_hi, x_lo = qn[side], qn[from_hi], qn[from_lo]
+        middle = [spread(x, first + 4 * t) for t in range(CY // 8)]
+        middle = jnp.concatenate(middle, axis=0)
+        return plane(middle, spread(x_hi, first), spread(x_lo, first + 4 * (CY // 8 - 1)))
+
+    ea = [[None, None] for _ in range(4)]
+    carry_plane = []
+    for c in range(2):
+        tile = pl.ds(c * 8, 8)
+        own = plane(q[c], qy_hi[tile, :], qy_lo[tile, :])
+        sides = (
+            (spread(own, CX - 2), beyond(0, 2, 4, c, 0)),
+            (spread(own, CX - 1), beyond(0, 2, 4, c, 1)),
+            (beyond(1, 3, 5, c, 2), spread(own, 0)),
+            (beyond(1, 3, 5, c, 3), spread(own, 1)),
+        )
+        for m, pair in enumerate(sides):
+            value = jnp.where(even, *pair) + grown[c][m]
+            ea[m][c] = jnp.where(level_ok, value, 0.0)
         around = (q[c][CY - 8 :], qy_hi[tile, :], qy_lo[tile, :], q[c][:8])
         turned = [turn(x, by, 0) for x, by in zip(around, (2, 2, -2, -2))]
         carry_plane.append(
@@ -648,7 +694,7 @@
         for c in range(3):
             a1_out[slot(c, CZ, EY), :] = jnp.zeros((EY, CX), jnp.float32)
 
-    for one in ups + sums + layers + faces + corners + columns:
+    for one in ups + sums + layers + faces + corners + columns + planes:
         one.wait_send()
 
 
@@ -732,9 +778,10 @@
     a1, v = pl.pallas_call(
         comm_kernel,
         out_shape=(f32(3 * (CZ + 2) * EY, CX), f32(2 * EY, CX)),
-        in_specs=[pl.BlockSpec(memory_space=pltpu.HBM), whole],
+        in_specs=[pl.BlockSpec(memory_space=pltpu.HBM)] * 2,
         out_specs=(whole,) * 2,
         scratch_shapes=[
+            vmem(CY, CX),
             vmem(2 * EZ * 8, CX),
             vmem(8 * (CZ + 2) * CY, CX),
             vmem(8 * (CZ + 2) * 8, CX),
@@ -753,20 +800,22 @@
             vmem(8 * (NY_DEV - 1), CX),
             vmem(CY * (NX_DEV - 1), CX),
             vmem(2 * CY, CX),
+            vmem(8, CX),
+            vmem(6, 8, CX),
             vmem(16, CX),
             vmem(16, CX),
             vmem(16, CX),
             vmem(16, CX),
         ]
         + [pltpu.SemaphoreType.REGULAR] * 3
-        + [dma((2,))]
+        + [dma((5,))]
         + [dma((NZ_DEV - 1,))] * 2
         + [dma((2, 2))] * 2
         + [dma((2,))] * 4
         + [dma((8,))] * 2
         + [dma((NY_DEV - 1,))] * 2
         + [dma((NX_DEV - 1,))] * 2
-        + [dma((2,))] * 2,
+        + [dma((8,))] * 2,
         compiler_params=pltpu.CompilerParams(
             collective_id=0, has_side_effects=True, vmem_limit_bytes=VMEM_BYTES
         ),

time: 24.4 us -> 23.4 us (0.959)
  the two profiles are of different devices: /device:TPU:193 before, /device:TPU:1 now
where the time goes in v5:
time: 23.4 us; the launch traced here: 23.3 us
  Pallas kernels  23.3 us (100%)
    pallas_call x1, Pallas kernels, local(): pl.pallas_call(comm_kernel, out_shape=(f32(3 * (CZ + 2) * EY, CX), f32(2...  19.5 us
    pallas_call x1, Pallas kernels, local(): pl.pallas_call(step_kernel, out_shape=f32(3 * CZ * CY, CX), in_specs=[who...  3.87 us

profile of v5, /device:TPU:1, one launch (start us, length us, event | category | flops | bytes accessed | tf_op | source)
XLA Modules:
  0.0 23.3 jit_solution(9243761361601301494)
XLA Ops:
  0.0 19.5 %exchange.1 = (f32[6000,128]{1,0:T(8,128)S(1)}, f32[80,128]{1,0:T(8,128)S(1)}) custom-call(f32[3072,128]{1,0:T(8,128)} %bitcast.2, f32[32,128]{1,0:T(8,128)} %mag_hbm.1), custom_call_target="tpu_custom_call" | custom-call | tf_op jit(solution)/shard_map/exchange/pallas_call | solution.py:778
  19.5 3.9 %steps.1 = f32[4608,128]{1,0:T(8,128)} custom-call(f32[6000,128]{1,0:T(8,128)S(1)} %get-tuple-element.7.a1, f32[80,128]{1,0:T(8,128)S(1)} %get-tuple-element.8.v_ref), custom_call_target="tpu_custom_call" | custom-call | tf_op jit(solution)/shard_map/steps/pallas_call | solution.py:824

commit v6 on v5

--- a/solution.py
+++ b/solution.py
@@ -74,6 +74,8 @@
     side_v,
     t_v,
     tr,
+    half_s,
+    half_r,
     ys_lo,
     ys_hi,
     yr_lo,
@@ -184,12 +186,14 @@
         return jnp.logical_or(place_z >= d, jnp.logical_and(gz == half, d == 1))
 
     higher = (
-        [dict(dz=d) for d in range(1, NZ_DEV)]
-        + [dict(dy=d) for d in range(1, NY_DEV)]
+        [dict(dy=d) for d in range(1, NY_DEV)]
         + [dict(dx=d) for d in range(1, NX_DEV)]
         + [dict(dy=1, dx=1), dict(dy=1, dx=-1)]
     )
-    heard, answers = gz + gy + gx, (half - 1 - place_z) + middle
+    heard = place_z + (gz >= half).astype(jnp.int32) + gy + gx
+    answers = (half - 1 - place_z) + middle
+    for d in range(1, half + 1):
+        tell(barrier, there(dz=d) & ((place_z + d < half) | (gz == half - 1)), dz=d)
     answers = answers + there(dy=1).astype(jnp.int32) + there(dx=1).astype(jnp.int32)
     others = jnp.maximum(NY_DEV - 2 - gy, 0) + jnp.maximum(NX_DEV - 2 - gx, 0)
     for by in higher:
@@ -211,14 +215,14 @@
     for load in loads:
         load.start()
     wait_for(barrier, heard)
+    for d in range(1, half):
+        tell(here_sem, there(dz=-d) & close(d), dz=-d)
+    for d in range(2, half + 1):
+        tell(far, gz == half - 1 + d, dz=-d)
     for by in higher:
         back = {k: -v for k, v in by.items()}
-        if "dz" in by:
-            tell(here_sem, there(**back) & close(by["dz"]), **back)
-            tell(far, there(**back) & jnp.logical_not(close(by["dz"])), **back)
-        else:
-            step = max(by.values())
-            tell(here_sem if step == 1 else wide, there(**back), **back)
+        step = max(by.values())
+        tell(here_sem if step == 1 else wide, there(**back), **back)
 
     def clear(by, *refs):
         @pl.when(jnp.logical_not(there(**by)))
@@ -276,15 +280,19 @@
     for one in layers:
         one.start()
 
-    ups = [
-        Hop(t_v, tr.at[d - 1], s_t.at[d - 1], r_t.at[d - 1], dz=d) for d in range(1, NZ_DEV)
+    ups = [Hop(t_v, tr.at[d - 1], s_t.at[d - 1], r_t.at[d - 1], dz=d) for d in range(1, half)]
+    for d, one in enumerate(ups, 1):
+        one.to = one.to & (place_z + d < half)
+        one.back = place_z >= d
+    across = [
+        Hop(half_s, half_r, s_t.at[half - 2 + d], r_t.at[half - 2 + d], dz=d)
+        for d in range(1, half + 1)
     ]
-
-    def near(d):
-        return jnp.logical_or(place_z + d < half, jnp.logical_and(gz == half - 1, d == 1))
-
-    for d, one in enumerate(ups, 1):
-        pl.when(one.to & near(d))(one.copy.start)
+    for d, one in enumerate(across, 1):
+        one.to = gz == half - 1
+        one.back = gz == half - 1 + d
+    for one in ups:
+        one.start()
 
     sums = [
         Hop(mc_s, mc_r.at[pl.ds(8 * (d - 1), 8)], s_mc.at[d - 1], r_mc.at[d - 1], dy=d)
@@ -340,13 +348,6 @@
     wait_for(wide, others)
     for one in sums:
         one.start()
-
-    @pl.when(gz < half)
-    def _():
-        pl.semaphore_wait(far, half - middle)
-
-    for d, one in enumerate(ups, 1):
-        pl.when(one.to & jnp.logical_not(near(d)))(one.copy.start)
 
     def slot(k, z, high):
         return pl.ds(pl.multiple_of((k * (CZ + 2) + z + 1) * high, 8), high)
@@ -427,6 +428,15 @@
     block = Strip(side_v, pre_m, CY)
     strip = Strip(ext_v, pre_e, 8)
     block_end = block.middle(UNROLL_PRE)
+
+    @pl.when(gz == half - 1)
+    def _():
+        for one in ups:
+            one.copy.wait_recv()
+        half_s[...] = (t_v[...] + tr[0]) + (tr[1] + tr[2])
+        pl.semaphore_wait(far, half - 1)
+        for one in across:
+            one.copy.start()
 
     col = mag
     row_of = rows((CY, CX))
@@ -497,18 +507,33 @@
 
     block.ends(*block_end)
 
-    for one in ups:
+    def raise_q(x):
+        q_v[pl.ds(0, CY), :] = q_v[pl.ds(0, CY), :] + spacing * x[CY:]
+        q_v[pl.ds(CY, CY), :] = q_v[pl.ds(CY, CY), :] - spacing * x[:CY]
+
+    for d, one in enumerate(ups, 1):
+        pl.when(one.back & (gz != half - 1))(one.copy.wait_recv)
 
         @pl.when(one.back)
-        def _(one=one):
-            one.wait_recv()
-
-    for d in range(1, NZ_DEV):
-
-        @pl.when(there(dz=-d))
         def _(d=d):
-            q_v[pl.ds(0, CY), :] = q_v[pl.ds(0, CY), :] + spacing * tr[d - 1, pl.ds(CY, CY), :]
-            q_v[pl.ds(CY, CY), :] = q_v[pl.ds(CY, CY), :] - spacing * tr[d - 1, pl.ds(0, CY), :]
+            raise_q(tr[d - 1])
+
+    for one in faces:
+        one.wait_recv()
+    for c in range(2):
+        for k in range(2):
+            here = pl.ds((2 * c + k) * CZ, CZ)
+            for j, ref in enumerate((ys_hi, yr_hi, yr_lo, ys_lo)):
+                ext_v[pl.ds((c * EZ + 1) * 8 + 2 * j + k, CZ, stride=8), :] = ref[here, :]
+
+    strip_end = strip.middle(UNROLL_STRIP)
+
+    for one in across:
+        one.wait_recv()
+
+    @pl.when(gz >= half)
+    def _():
+        raise_q(half_r[...])
 
     q = tuple(q_v[pl.ds(c * CY, CY), :] for c in range(2))
     lane8 = lanes((8, CX))
@@ -546,14 +571,6 @@
 
     lax.fori_loop(-1, CZ + 1, finish_block, 0, unroll=UNROLL_POST)
 
-    for one in faces:
-        one.wait_recv()
-    for c in range(2):
-        for k in range(2):
-            here = pl.ds((2 * c + k) * CZ, CZ)
-            for j, ref in enumerate((ys_hi, yr_hi, yr_lo, ys_lo)):
-                ext_v[pl.ds((c * EZ + 1) * 8 + 2 * j + k, CZ, stride=8), :] = ref[here, :]
-
     for one in corners:
         one.wait_recv()
     for c in range(2):
@@ -562,7 +579,7 @@
             of = pl.ds((c * 3 + i) * 2, 2)
             for j, ref in enumerate((cs_hi, cr_hi, cr_lo, cs_lo)):
                 ext_v[pl.ds(first + 2 * j, 2), :] = ref[of, :]
-    strip.ends(*strip.middle(UNROLL_STRIP))
+    strip.ends(*strip_end)
 
     row8 = rows((8, CX))
 
@@ -694,7 +711,7 @@
         for c in range(3):
             a1_out[slot(c, CZ, EY), :] = jnp.zeros((EY, CX), jnp.float32)
 
-    for one in ups + sums + layers + faces + corners + columns + planes:
+    for one in ups + across + sums + layers + faces + corners + columns + planes:
         one.wait_send()
 
 
@@ -787,7 +804,9 @@
             vmem(8 * (CZ + 2) * 8, CX),
             vmem(2 * LEVEL, CX),
             vmem(2 * CY, CX),
-            vmem(NZ_DEV - 1, 2 * CY, CX),
+            vmem(NZ_DEV // 2 - 1, 2 * CY, CX),
+            vmem(2 * CY, CX),
+            vmem(2 * CY, CX),
         ]
         + [vmem(4 * CZ, CX)] * 4
         + [vmem(16, CX)] * 4

time: 23.4 us -> 23.5 us (level)
  the two profiles are of different devices: /device:TPU:1 before, /device:TPU:193 now
where the time goes in v6:
time: 23.5 us; the launch traced here: 23.4 us
  Pallas kernels  23.4 us (100%)
    pallas_call x1, Pallas kernels, local(): pl.pallas_call(comm_kernel, out_shape=(f32(3 * (CZ + 2) * EY, CX), f32(2...  19.5 us
    pallas_call x1, Pallas kernels, local(): pl.pallas_call(step_kernel, out_shape=f32(3 * CZ * CY, CX), in_specs=[who...  3.87 us

profile of v6, /device:TPU:193, one launch (start us, length us, event | category | flops | bytes accessed | tf_op | source)
XLA Modules:
  0.0 23.4 jit_solution(142031507117209696)
XLA Ops:
  0.0 19.5 %exchange.1 = (f32[6000,128]{1,0:T(8,128)S(1)}, f32[80,128]{1,0:T(8,128)S(1)}) custom-call(f32[3072,128]{1,0:T(8,128)} %bitcast.2, f32[32,128]{1,0:T(8,128)} %mag_hbm.1), custom_call_target="tpu_custom_call" | custom-call | tf_op jit(solution)/shard_map/exchange/pallas_call | solution.py:795
  19.5 3.9 %steps.1 = f32[4608,128]{1,0:T(8,128)} custom-call(f32[6000,128]{1,0:T(8,128)S(1)} %get-tuple-element.7.a1, f32[80,128]{1,0:T(8,128)S(1)} %get-tuple-element.8.v_ref), custom_call_target="tpu_custom_call" | custom-call | tf_op jit(solution)/shard_map/steps/pallas_call | solution.py:843

commit v7 on v6

--- a/solution.py
+++ b/solution.py
@@ -277,8 +277,6 @@
                 dz=-1,
             )
         )
-    for one in layers:
-        one.start()
 
     ups = [Hop(t_v, tr.at[d - 1], s_t.at[d - 1], r_t.at[d - 1], dz=d) for d in range(1, half)]
     for d, one in enumerate(ups, 1):
@@ -292,6 +290,8 @@
         one.to = gz == half - 1
         one.back = gz == half - 1 + d
     for one in ups:
+        one.start()
+    for one in layers:
         one.start()
 
     sums = [

time: 23.5 us -> 22.7 us (0.966)
  the two profiles are of different devices: /device:TPU:193 before, /device:TPU:1 now
where the time goes in v7:
time: 22.7 us; the launch traced here: 22.6 us
  Pallas kernels  22.6 us (100%)
    pallas_call x1, Pallas kernels, local(): pl.pallas_call(comm_kernel, out_shape=(f32(3 * (CZ + 2) * EY, CX), f32(2...  18.7 us
    pallas_call x1, Pallas kernels, local(): pl.pallas_call(step_kernel, out_shape=f32(3 * CZ * CY, CX), in_specs=[who...  3.87 us

profile of v7, /device:TPU:1, one launch (start us, length us, event | category | flops | bytes accessed | tf_op | source)
XLA Modules:
  0.0 22.6 jit_solution(9972538709505657057)
XLA Ops:
  0.0 18.7 %exchange.1 = (f32[6000,128]{1,0:T(8,128)S(1)}, f32[80,128]{1,0:T(8,128)S(1)}) custom-call(f32[3072,128]{1,0:T(8,128)} %bitcast.2, f32[32,128]{1,0:T(8,128)} %mag_hbm.1), custom_call_target="tpu_custom_call" | custom-call | tf_op jit(solution)/shard_map/exchange/pallas_call | solution.py:795
  18.7 3.9 %steps.1 = f32[4608,128]{1,0:T(8,128)} custom-call(f32[6000,128]{1,0:T(8,128)S(1)} %get-tuple-element.7.a1, f32[80,128]{1,0:T(8,128)S(1)} %get-tuple-element.8.v_ref), custom_call_target="tpu_custom_call" | custom-call | tf_op jit(solution)/shard_map/steps/pallas_call | solution.py:843
